TPU v7x, 32 devices: a whole 2x2x4 slice. The times are simulated.
32 devices in a mesh: row: 4 (over x, core), col: 8 (over z, y).
Axes of the slice: x: 2, y: 2, z: 4, core: 2. Of those that a mesh axis runs over, the one named last changes fastest.
Arguments:
- front_matrix: float32 [32, 4, 128, 16, 8, 128], P(None, 'row', None, None, 'col'), as said below
- children: bfloat16 [2, 4, 4, 128, 16, 8, 128], P(None, None, 'row', None, None, 'col'), may hold values from -0.5 to 0.5
- child_map: int32 [2, 16], replicated, may hold values from 0 to 127, as said below
- row_order: int32 [2, 16, 128], replicated, may hold values from 0 to 127, each once within a row
Outputs:
- schur_part: float32 [32, 4, 128, 16, 8, 128], P(None, 'row', None, None, 'col')
- factor_part: float32 [32, 4, 128, 1536], P('col', 'row')
Inputs may be any that keep to these rules, and one draw needn't show every extreme that they name: `front_matrix`: Off-diagonal entries lie within -1.2 and 1.2 + 0.3 * sqrt(16384); diagonal entries lie between 2.5 and 3.9 times the square root of 16384. The lower triangle, with the children's rows added and mirrored, is positive definite. `child_map`: each child sends its tile rows to distinct front tile rows. Of the 4 tile rows of one child held by one device row, at most 2 go to any one device row (front tile row modulo 4), and exactly 2 go to some device row.
All inputs are finite; a program needn't handle non-finite values.
Results may differ from a plain program's by a relative error of at most 0.001.
Values may be sent and summed in bfloat16 or wider, within the bound.
No kernel may reach another device: no remote copies, remote signals or barrier semaphores. Data moves between devices by JAX's collectives and lax.ppermute only.
A program may use at most 384 MiB of HBM per device.

v0:
```python
import jax
import jax.numpy as jnp
from jax import lax
from jax.sharding import PartitionSpec as P

PWT = 4
STEPS = 3
CAP = 2


def from_root(value, axis, source):
    kept = jnp.where(lax.axis_index(axis) == source, value, 0).astype(value.dtype)
    return lax.psum(kept, axis)


def slot_ranks(mapping, row_count):
    indices = jnp.arange(mapping.shape[0], dtype=jnp.int32)
    sources = indices % row_count
    targets = mapping % row_count
    earlier = (
        (sources[:, None] == sources[None, :])
        & (targets[:, None] == targets[None, :])
        & (indices[None, :] < indices[:, None])
    )
    return (sources, targets, jnp.sum(earlier.astype(jnp.int32), axis=1))


def pack_child(rows_local, ordering, targets, rank_in_group, row_count, row_dev):
    local_count, tile_size, width_local = rows_local.shape
    own_ids = jnp.arange(local_count, dtype=jnp.int32) * row_count + row_dev
    own_order = ordering[own_ids]
    onehot_rows = (
        own_order[:, :, None] == jnp.arange(tile_size, dtype=jnp.int32)[None, None, :]
    ).astype(jnp.bfloat16)
    moved_rows = jnp.einsum(
        "atr,atx->arx", onehot_rows, rows_local, preferred_element_type=jnp.float32
    ).astype(jnp.bfloat16)
    slot_of = targets[own_ids] * CAP + rank_in_group[own_ids]
    selector = (jnp.arange(row_count * CAP, dtype=jnp.int32)[:, None] == slot_of[None, :]).astype(
        jnp.bfloat16
    )
    packed = jnp.einsum(
        "ja,arx->jrx", selector, moved_rows, preferred_element_type=jnp.float32
    ).astype(jnp.bfloat16)
    return packed.reshape(row_count, CAP, tile_size, width_local)


def unpack_selector(mapping, sources, targets, rank_in_group, row_count, row_dev, local_rows):
    slot_of = sources * CAP + rank_in_group
    landing = (
        (mapping // row_count)[:, None] == jnp.arange(local_rows, dtype=jnp.int32)[None, :]
    ) & (targets == row_dev)[:, None]
    arrival = slot_of[:, None] == jnp.arange(row_count * CAP, dtype=jnp.int32)[None, :]
    return jnp.dot(
        landing.astype(jnp.bfloat16).T,
        arrival.astype(jnp.bfloat16),
        preferred_element_type=jnp.float32,
    ).astype(jnp.bfloat16)


def place_rows(matrix_rows, selector, received):
    flat_slots = received.reshape(selector.shape[1], received.shape[2], received.shape[3])
    return matrix_rows + jnp.einsum(
        "aj,jtx->atx", selector, flat_slots, preferred_element_type=jnp.float32
    )


def current_tile(matrix, factors, copies, local_col, tile_size):
    owned = matrix[:, :, local_col * tile_size : (local_col + 1) * tile_size]
    for earlier_index in range(len(factors)):
        owned = owned - jnp.einsum(
            "atk,uk->atu",
            factors[earlier_index],
            copies[earlier_index][local_col],
            precision=lax.Precision.HIGHEST,
            preferred_element_type=jnp.float32,
        )
    return owned


def shards(front_matrix, children, child_map, row_order):
    row_count = lax.axis_size("row")
    col_count = lax.axis_size("col")
    row_dev = lax.axis_index("row")
    col_dev = lax.axis_index("col")
    local_rows = front_matrix.shape[0]
    tile_size = front_matrix.shape[2]
    local_cols = front_matrix.shape[3]
    width_local = local_cols * tile_size
    panel_width = PWT * tile_size
    matrix = front_matrix.reshape(local_rows, tile_size, width_local)
    packed = []
    selectors = []
    for child_index in range(2):
        sources, targets, rank_in_group = slot_ranks(child_map[child_index], row_count)
        rows_local = children[child_index].reshape(children.shape[1], tile_size, width_local)
        packed.append(
            pack_child(
                rows_local, row_order[child_index], targets, rank_in_group, row_count, row_dev
            )
        )
        selectors.append(
            unpack_selector(
                child_map[child_index],
                sources,
                targets,
                rank_in_group,
                row_count,
                row_dev,
                local_rows,
            )
        )
    received = (
        lax.all_to_all(packed[0], "row", split_axis=0, concat_axis=0, tiled=True),
        lax.all_to_all(packed[1], "row", split_axis=0, concat_axis=0, tiled=True),
    )
    for child_index in range(2):
        matrix = place_rows(matrix, selectors[child_index], received[child_index])
    pending = []
    row_tiles = jnp.arange(local_rows, dtype=jnp.int32) * row_count + row_dev
    col_tiles = jnp.arange(local_cols, dtype=jnp.int32) * col_count + col_dev
    factors = []
    copies = []
    for panel_index in range(STEPS):
        first_tile = panel_index * PWT
        pieces = []
        for offset in range(PWT):
            tile_col = first_tile + offset
            local_col = tile_col // col_count
            owned = current_tile(matrix, factors, copies, local_col, tile_size)
            pieces.append(from_root(owned, "col", tile_col % col_count))
        panel_cols = jnp.concatenate(pieces, axis=2)
        blocks = []
        for offset in range(PWT):
            tile_row = first_tile + offset
            blocks.append(from_root(panel_cols[tile_row // row_count], "row", tile_row % row_count))
        diagonal = jnp.concatenate(blocks, axis=0)
        mirrored = jnp.tril(diagonal) + jnp.tril(diagonal, -1).T
        cholesky_factor = jnp.linalg.cholesky(mirrored)
        flat_cols = panel_cols.reshape(local_rows * tile_size, panel_width)
        solved = jax.scipy.linalg.solve_triangular(
            cholesky_factor, flat_cols.T, lower=True
        ).T.reshape(local_rows, tile_size, panel_width)
        diag_rows = cholesky_factor.reshape(PWT, tile_size, panel_width)[
            jnp.clip(row_tiles - first_tile, 0, PWT - 1)
        ]
        inside = (row_tiles >= first_tile) & (row_tiles < first_tile + PWT)
        factor = jnp.where(inside[:, None, None], diag_rows, solved)
        factor = jnp.where((row_tiles < first_tile)[:, None, None], jnp.zeros_like(factor), factor)
        picked = factor[col_tiles // row_count]
        factor_cols = from_root(picked.astype(jnp.bfloat16), "row", col_dev % row_count).astype(
            picked.dtype
        )
        factors.append(factor)
        copies.append(factor_cols)
    stacked = jnp.concatenate(factors, axis=2)
    stacked_cols = jnp.concatenate(copies, axis=2)
    update = jnp.einsum(
        "atk,buk->atbu",
        stacked,
        stacked_cols,
        precision=lax.Precision.HIGHEST,
        preferred_element_type=jnp.float32,
    )
    final_rows = matrix.reshape(local_rows, tile_size, local_cols, tile_size) - update
    kept_mask = (row_tiles[:, None] >= col_tiles[None, :]) & (col_tiles[None, :] >= STEPS * PWT)
    schur_part = jnp.where(
        kept_mask[:, None, :, None], final_rows, jnp.zeros_like(final_rows)
    ).reshape(front_matrix.shape)
    share_rows = local_rows // col_count
    factor_part = lax.dynamic_slice_in_dim(stacked, col_dev * share_rows, share_rows, 0).reshape(
        share_rows, 1, tile_size, STEPS * panel_width
    )
    return (schur_part, factor_part)


def solution(mesh):
    placed = (
        P(None, "row", None, None, "col", None),
        P(None, None, "row", None, None, "col", None),
        P(),
        P(),
    )
    return jax.shard_map(
        shards,
        mesh=mesh,
        in_specs=placed,
        out_specs=(P(None, "row", None, None, "col", None), P("col", "row", None, None)),
        check_vma=False,
    )
```

profile of v0, /device:TPU:24, one launch (start us, length us, event | category | flops | bytes accessed | tf_op | source)
XLA Modules:
  0.0 2240.5 jit_solution(8669075045916751442)
XLA Ops:
  67.1 24.2 %all-to-all-done.1 = bf16[4,2,128,2048]{3,1,2,0:T(2,128)(2,1)} async-done(((bf16[4,2,128,2048]{3,1,2,0:T(2,128)(2,1)}), bf16[4,2,128,2048]{3,1,2,0:T(2,128)(2,1)}, u32[]{:S(2)}, u32[]{:S(2)}) %all-to-all-start.1) | async-done | bytes 4194336 | tf_op jit(solution)/shard_map/all_to_all | solution.py:115
  96.7 92.9 %reduce.19 = f32[32,128,16,128]{3,2,1,0:T(8,128)} reduce(f32[32,1,128,16,1,128]{5,4,3,2,1,0:T(1,128)} %param.7, f32[]{:T(128)} %broadcast.1002), dimensions={1,4}, to_apply=%param.7.reduce_sub_computation.3 | reduce | bytes 67108864 | tf_op args[0]
  189.7 35.5 %reshape.502 = f32[32,128,2048]{2,1,0:T(8,128)} reshape(f32[32,128,16,128]{3,2,1,0:T(8,128)} %reduce.19) | data formatting | bytes 67108864 | tf_op jit(solution)/shard_map/reshape | solution.py:91
  258.3 15.9 fusion.63
  274.2 14.9 fusion.64
  289.1 67.2 %copy_add_fusion = f32[32,128,2048]{2,1,0:T(8,128)} fusion(f32[32,128,2048]{2,0,1:T(8,128)} %fusion.63, f32[32,128,2048]{2,1,0:T(8,128)} %reshape.502, f32[32,128,2048]{2,0,1:T(8,128)} %fusion.64), kind=kLoop, calls=%fused_computation.21 | loop fusion | flops 16777216 | bytes 134217728 | tf_op jit(solution)/shard_map/add | solution.py:63
  361.8 271.2 %all-reduce.27.cloned.1.call-done = (f32[32,128,128]{2,1,0:T(8,128)}, f32[32,128,128]{2,1,0:T(8,128)}, f32[32,128,128]{2,1,0:T(8,128)}, f32[32,128,128]{2,1,0:T(8,128)}) async-done(((f32[32,128,128]{2,1,0:T(8,128)}, f32[32,128,128]{2,1,0:T(8,128)}, f32[32,128,128]{2,1,0:T(8,128)}, f32[32,128,128]{2,1,0:T(8,128)}), (f32[32,128,128]{2,1,0:T(8,128)}, f32[32,128,128]{2,1,0:T(8,128)}, f32[32,128,128]{2,1,0:T(8,128)}, ...) | async-done | bytes 8388624 | tf_op jit(solution)/shard_map/psum | solution.py:13
  652.5 28.9 %all-reduce.33.cloned.1.call-done = (f32[128,512]{1,0:T(8,128)}, f32[128,512]{1,0:T(8,128)}, f32[128,512]{1,0:T(8,128)}, f32[128,512]{1,0:T(8,128)}) async-done(((f32[128,512]{1,0:T(8,128)}, f32[128,512]{1,0:T(8,128)}, f32[128,512]{1,0:T(8,128)}, f32[128,512]{1,0:T(8,128)}), (f32[128,512]{1,0:T(8,128)}, f32[128,512]{1,0:T(8,128)}, f32[128,512]{1,0:T(8,128)}, ...) | async-done | bytes 1048592 | tf_op jit(solution)/shard_map/psum | solution.py:13
  792.7 39.3 %custom-call.34 = f32[4,128,128]{1,2,0:T(8,128)S(1)} custom-call(f32[4,128,128]{2,1,0:T(8,128)S(1)} %get-tuple-element.24), custom_call_target="InvertDiagBlocksLowerTriangular" | custom-call | tf_op jit(solution)/shard_map/jit(_solve_triangular)/triangular_solve | solution.py:141
  906.9 34.8 %all-reduce.17.cloned.1.call-done = bf16[16,128,512]{2,1,0:T(8,128)(2,1)} async-done(((bf16[16,128,512]{2,1,0:T(8,128)(2,1)}), bf16[16,128,512]{2,1,0:T(8,128)(2,1)}) %all-reduce.17.cloned.1.call-update) | async-done | bytes 2097168 | tf_op jit(solution)/shard_map/psum | solution.py:13
  953.2 269.9 %all-reduce.25.cloned.1.call-done = (f32[32,128,128]{2,1,0:T(8,128)}, f32[32,128,128]{2,1,0:T(8,128)}, f32[32,128,128]{2,1,0:T(8,128)}, f32[32,128,128]{2,1,0:T(8,128)}) async-done(((f32[32,128,128]{2,1,0:T(8,128)}, f32[32,128,128]{2,1,0:T(8,128)}, f32[32,128,128]{2,1,0:T(8,128)}, f32[32,128,128]{2,1,0:T(8,128)}), (f32[32,128,128]{2,1,0:T(8,128)}, f32[32,128,128]{2,1,0:T(8,128)}, f32[32,128,128]{2,1,0:T(8,128)}, ...) | async-done | bytes 8388624 | tf_op jit(solution)/shard_map/psum | solution.py:13
  1250.9 20.6 all-reduce.31.cloned.1.call-done
  1343.6 11.9 cholesky.503
  1382.4 39.3 %custom-call.38 = f32[4,128,128]{1,2,0:T(8,128)S(1)} custom-call(f32[4,128,128]{2,1,0:T(8,128)S(1)} %get-tuple-element.25), custom_call_target="InvertDiagBlocksLowerTriangular" | custom-call | tf_op jit(solution)/shard_map/jit(_solve_triangular)/triangular_solve | solution.py:141
  1460.1 12.0 select_select_fusion.2
  1496.7 35.0 %all-reduce.19.cloned.1.call-done = bf16[16,128,512]{2,1,0:T(8,128)(2,1)} async-done(((bf16[16,128,512]{2,1,0:T(8,128)(2,1)}), bf16[16,128,512]{2,1,0:T(8,128)(2,1)}) %all-reduce.19.cloned.1.call-update) | async-done | bytes 2097168 | tf_op jit(solution)/shard_map/psum | solution.py:13
  1543.6 269.5 %all-reduce.23.cloned.1.call-done = (f32[32,128,128]{2,1,0:T(8,128)}, f32[32,128,128]{2,1,0:T(8,128)}, f32[32,128,128]{2,1,0:T(8,128)}, f32[32,128,128]{2,1,0:T(8,128)}) async-done(((f32[32,128,128]{2,1,0:T(8,128)}, f32[32,128,128]{2,1,0:T(8,128)}, f32[32,128,128]{2,1,0:T(8,128)}, f32[32,128,128]{2,1,0:T(8,128)}), (f32[32,128,128]{2,1,0:T(8,128)}, f32[32,128,128]{2,1,0:T(8,128)}, f32[32,128,128]{2,1,0:T(8,128)}, ...) | async-done | bytes 8388624 | tf_op jit(solution)/shard_map/psum | solution.py:13
  1832.5 29.0 %all-reduce.29.cloned.1.call-done = (f32[128,512]{1,0:T(8,128)}, f32[128,512]{1,0:T(8,128)}, f32[128,512]{1,0:T(8,128)}, f32[128,512]{1,0:T(8,128)}) async-done(((f32[128,512]{1,0:T(8,128)}, f32[128,512]{1,0:T(8,128)}, f32[128,512]{1,0:T(8,128)}, f32[128,512]{1,0:T(8,128)}), (f32[128,512]{1,0:T(8,128)}, f32[128,512]{1,0:T(8,128)}, f32[128,512]{1,0:T(8,128)}, ...) | async-done | bytes 1048592 | tf_op jit(solution)/shard_map/psum | solution.py:13
  1933.8 11.9 cholesky.575
  1959.2 39.3 %custom-call.42 = f32[4,128,128]{1,2,0:T(8,128)S(1)} custom-call(f32[4,128,128]{2,1,0:T(8,128)S(1)} %get-tuple-element.26), custom_call_target="InvertDiagBlocksLowerTriangular" | custom-call | tf_op jit(solution)/shard_map/jit(_solve_triangular)/triangular_solve | solution.py:141
  2038.5 12.1 select_select_fusion
  2067.8 40.3 %all-reduce.21.cloned.1.call-done = bf16[16,128,512]{2,1,0:T(8,128)(2,1)} async-done(((bf16[16,128,512]{2,1,0:T(8,128)(2,1)}), bf16[16,128,512]{2,1,0:T(8,128)(2,1)}) %all-reduce.21.cloned.1.call-update) | async-done | bytes 2097168 | tf_op jit(solution)/shard_map/psum | solution.py:13
  2108.0 87.0 %fusion.1 = f32[32,1,128,16,1,128]{5,2,3,0,4,1:T(8,128)} fusion(pred[32,16]{1,0:T(8,128)(4,1)S(1)} %compare_and_fusion, bf16[16,128,512]{2,1,0:T(8,128)(2,1)} %all-reduce.21.cloned.1.call-done, bf16[16,128,512]{2,1,0:T(8,128)(2,1)} %all-reduce.19.cloned.1.call-done, bf16[16,128,512]{2,1,0:T(8,128)(2,1)S(1)} %copy-done.19, ...), kind=kOutput, calls=%fused_computation.20 | convolution fusion | flops 154667057152 | bytes 98566656 | tf_op jit(solution)/shard_map/atk,buk->atbu/dot_general | solution.py:158
  2195.0 38.6 %copy.107 = f32[32,1,128,16,1,128]{5,4,3,2,1,0:T(1,128)} copy(f32[32,1,128,16,1,128]{5,2,3,0,4,1:T(8,128)} %fusion.1) | data formatting | bytes 67108864
  (331 shorter events, 700.6 us)
Async XLA Ops:
  13.7 2.8 copy-start.20
  38.0 53.3 %all-to-all-start.1 = ((bf16[4,2,128,2048]{3,1,2,0:T(2,128)(2,1)}), bf16[4,2,128,2048]{3,1,2,0:T(2,128)(2,1)}, u32[]{:S(2)}, u32[]{:S(2)}) async-start(bf16[4,2,128,2048]{3,1,2,0:T(2,128)(2,1)} %copy.83), calls=%async_computation.1 | async-start | bytes 8388608 | tf_op jit(solution)/shard_map/all_to_all | solution.py:115
  91.3 150.5 %all-to-all-start = ((bf16[4,2,128,2048]{3,1,2,0:T(2,128)(2,1)}), bf16[4,2,128,2048]{3,1,2,0:T(2,128)(2,1)}, u32[]{:S(2)}, u32[]{:S(2)}) async-start(bf16[4,2,128,2048]{3,1,2,0:T(2,128)(2,1)} %copy.79), calls=%async_computation | async-start | bytes 8388608 | tf_op jit(solution)/shard_map/all_to_all | solution.py:114
  96.2 536.9 %all-reduce.27.cloned.1.call-start = ((), (), s32[]{:S(2)}) async-start(), calls=%async_computation.7 | async-start | bytes 16777216 | tf_op jit(solution)/shard_map/psum | solution.py:13
  189.7 35.5 %copy-start.21 = (s32[2,16]{1,0:T(2,128)S(1)}, s32[2,16]{1,0:T(2,128)}, u32[]{:S(2)}) copy-start(s32[2,16]{1,0:T(2,128)} %param.9) | copy-start | bytes 388
  361.7 319.8 %all-reduce.33.cloned.1.call-start = ((), (), s32[]{:S(2)}) async-start(), calls=%async_computation.10 | async-start | bytes 2097152 | tf_op jit(solution)/shard_map/psum | solution.py:13
  633.1 2.2 copy-start.12
  638.7 3.4 copy-start.6
  643.2 298.5 %all-reduce.17.cloned.1.call-start = ((), (), s32[]{:S(2)}) async-start(), calls=%async_computation.2 | async-start | bytes 4194304 | tf_op jit(solution)/shard_map/psum | solution.py:13
  841.0 15.1 copy-start
  847.7 8.4 copy-start.2
  889.0 334.1 %all-reduce.25.cloned.1.call-start = ((), (), s32[]{:S(2)}) async-start(), calls=%async_computation.6 | async-start | bytes 16777216 | tf_op jit(solution)/shard_map/psum | solution.py:13
  953.0 318.5 %all-reduce.31.cloned.1.call-start = ((), (), s32[]{:S(2)}) async-start(), calls=%async_computation.9 | async-start | bytes 2097152 | tf_op jit(solution)/shard_map/psum | solution.py:13
  1223.1 2.2 copy-start.18
  1228.8 3.4 copy-start.7
  1233.2 298.5 %all-reduce.19.cloned.1.call-start = ((), (), s32[]{:S(2)}) async-start(), calls=%async_computation.3 | async-start | bytes 4194304 | tf_op jit(solution)/shard_map/psum | solution.py:13
  1430.7 15.3 copy-start.1
  1437.4 8.6 copy-start.3
  1479.0 334.2 %all-reduce.23.cloned.1.call-start = ((), (), s32[]{:S(2)}) async-start(), calls=%async_computation.5 | async-start | bytes 16777216 | tf_op jit(solution)/shard_map/psum | solution.py:13
  1487.5 44.3 %copy-start.9 = (f32[32,128,128]{2,1,0:T(8,128)S(1)}, f32[32,128,128]{2,1,0:T(8,128)}, u32[]{:S(2)}) copy-start(f32[32,128,128]{2,1,0:T(8,128)} %fusion.83) | copy-start | bytes 6291460
  1543.0 318.5 %all-reduce.29.cloned.1.call-start = ((), (), s32[]{:S(2)}) async-start(), calls=%async_computation.8 | async-start | bytes 2097152 | tf_op jit(solution)/shard_map/psum | solution.py:13
  1818.8 3.4 copy-start.8
  1823.2 284.8 %all-reduce.21.cloned.1.call-start = ((), (), s32[]{:S(2)}) async-start(), calls=%async_computation.4 | async-start | bytes 4194304 | tf_op jit(solution)/shard_map/psum | solution.py:13
  2065.9 42.2 %copy-start.19 = (bf16[16,128,512]{2,1,0:T(8,128)(2,1)S(1)}, bf16[16,128,512]{2,1,0:T(8,128)(2,1)}, u32[]{:S(2)}) copy-start(bf16[16,128,512]{2,1,0:T(8,128)(2,1)} %all-reduce.17.cloned.1.call-done) | copy-start | bytes 6291460
  (9 other events, 14.4 us)
Sparse Core Ops, SparseCore 0:
  361.8 271.2 all-reduce.26
  643.3 38.0 all-reduce.32
  889.1 52.5 all-reduce.16
  953.1 269.9 all-reduce.24
  1233.3 38.0 all-reduce.30
  1479.1 52.5 all-reduce.18
  1543.1 269.9 all-reduce.22
  1823.3 38.0 all-reduce.28
  2056.3 51.7 all-reduce.20
where the time goes:
time: 2250 us; the launch traced here: 2240 us
  waiting for transfers between devices  1020 us (45%)
  other arithmetic  608 us (27%)
  local copies, waits for them, and re-layouts  342 us (15%)
  matrix products  234 us (10%)
  between operations  23.2 us (1%)
    psum x9, waiting for transfers between devices, from_root(): return lax.psum(kept, axis)  999 us
    another operation x45, other arithmetic, shards(): cholesky_factor = jnp.linalg.cholesky(mirrored)  239 us
    another operation x7, other arithmetic, shards(): jax.scipy.linalg.solve_triangular(cholesky_factor, flat_cols.T, lower=True)  119 us
    unnamed x1, other arithmetic  92.9 us
    dot_general x1, matrix products, shards(): jnp.einsum('atk,buk->atbu', stacked, stacked_cols, precision=lax.Precisio...  87 us
    unnamed x64, local copies, waits for them, and re-layouts  76.8 us
    another operation x21, matrix products, shards(): jax.scipy.linalg.solve_triangular(cholesky_factor, flat_cols.T, lower=True)  70.8 us
    add x1, other arithmetic, place_rows(): matrix_rows + jnp.einsum('aj,jtx->atx', selector, flat_slots, preferred_e...  67.2 us
  transfers between devices with their start and end apart: 11, of which 10 were waited for; matrix products, arithmetic and copies ran while one was open for 11% of the time, Pallas kernels for 0%

commit v1 on v0

v1 whole, which is shorter than its diff:
```python
import functools

import jax
import jax.numpy as jnp
from jax import lax
from jax.experimental import pallas as pl
from jax.experimental.pallas import tpu as pltpu
from jax.sharding import PartitionSpec as P

PWT = 4
STEPS = 3
CAP = 2
TILES = PWT * STEPS
F32 = jnp.float32
BF16 = jnp.bfloat16
LINK = jnp.float16
VMEM_LIMIT = 60 * 1024 * 1024


def slot_ranks(mapping, row_count):
    indices = jnp.arange(mapping.shape[0], dtype=jnp.int32)
    sources = indices % row_count
    targets = mapping % row_count
    earlier = (
        (sources[:, None] == sources[None, :])
        & (targets[:, None] == targets[None, :])
        & (indices[None, :] < indices[:, None])
    )
    return (sources, targets, jnp.sum(earlier.astype(jnp.int32), axis=1))


def dot(a, b, contract):
    return lax.dot_general(a, b, (contract, ((), ())), preferred_element_type=F32)


NT = ((1,), (1,))
NN = ((1,), (0,))
TN = ((0,), (0,))


def halves(x):
    high = x.astype(BF16)
    return high, (x - high.astype(F32)).astype(BF16)


def dot3(a, b, contract):
    ah, al = halves(a)
    bh, bl = halves(b)
    return dot(ah, bh, contract) + (dot(al, bh, contract) + dot(ah, bl, contract))


def spread_lane(x, j):
    return jnp.broadcast_to(x[:, j : j + 1], (8, x.shape[1]))


def spread_row(x, i):
    return jnp.broadcast_to(x[i : i + 1, :], (8, x.shape[1]))


def factor_tile(tile):
    size = tile.shape[0]
    sub = lax.broadcasted_iota(jnp.int32, (8, size), 0)
    lane = lax.broadcasted_iota(jnp.int32, (8, size), 1)
    groups = size // 8
    left = [tile[8 * s : 8 * s + 8] for s in range(groups)]
    right = [jnp.where(lane == sub + 8 * s, 1.0, 0.0).astype(F32) for s in range(groups)]
    for s in range(groups):
        columns = [spread_lane(left[s], 8 * s + b) for b in range(8)]
        square = {(a, b): spread_row(columns[b], a) for a in range(8) for b in range(a + 1)}
        lrow = [spread_row(left[s], i) for i in range(8)]
        rrow = [spread_row(right[s], i) for i in range(8)]
        new_left = jnp.zeros((8, size), F32)
        new_right = jnp.zeros((8, size), F32)
        for i in range(8):
            inverse = lax.rsqrt(square[i, i])
            below = {a: square[a, i] * inverse for a in range(i + 1, 8)}
            lrow[i] = lrow[i] * inverse
            rrow[i] = rrow[i] * inverse
            for a in range(i + 1, 8):
                for b in range(i + 1, a + 1):
                    square[a, b] = square[a, b] - below[a] * below[b]
                lrow[a] = lrow[a] - below[a] * lrow[i]
                rrow[a] = rrow[a] - below[a] * rrow[i]
            new_left = jnp.where(sub == i, lrow[i], new_left)
            new_right = jnp.where(sub == i, rrow[i], new_right)
        left[s], right[s] = new_left, new_right
        if s < groups - 1:
            turned = new_left.T
            for t in range(s + 1, groups):
                for a in range(8):
                    scale = jnp.broadcast_to(turned[8 * t : 8 * t + 8, a : a + 1], (8, size))
                    left[t] = left[t] - scale * lrow[a]
                    right[t] = right[t] - scale * rrow[a]
    return jnp.concatenate(left, 0), jnp.concatenate(right, 0)


def whole(shape):
    return pl.BlockSpec(shape, lambda *_: (0,) * len(shape), pipeline_mode=pl.Buffered(1))


def pack_kernel(row_count, ids_ref, map_ref, kids_ref, out_ref):
    out_ref[...] = jnp.zeros(out_ref.shape, out_ref.dtype)
    for h in range(2):
        targets = []
        for i in range(kids_ref.shape[1]):
            target = map_ref[h, i * row_count + ids_ref[0]] % row_count
            rank = jnp.int32(0)
            for earlier in targets:
                rank = rank + (earlier == target).astype(jnp.int32)
            targets.append(target)
            out_ref[target, h, rank] = kids_ref[h, i]


def pack_children(ids, child_map, kids, row_count):
    return pl.pallas_call(
        functools.partial(pack_kernel, row_count),
        out_shape=jax.ShapeDtypeStruct((row_count, 2, CAP) + kids.shape[2:], kids.dtype),
        grid_spec=pltpu.PrefetchScalarGridSpec(
            num_scalar_prefetch=2,
            grid=(1,),
            in_specs=[whole(kids.shape)],
            out_specs=whole((row_count, 2, CAP) + kids.shape[2:]),
        ),
        compiler_params=pltpu.CompilerParams(vmem_limit_bytes=VMEM_LIMIT),
    )(ids, child_map, kids)


def panel_kernel(lpc, share, slot_ref, *refs):
    fronts = refs[:lpc]
    order_ref, recv_ref, high_ref, low_ref = refs[lpc:]
    tile = high_ref.shape[-1]
    rows = lax.broadcasted_iota(jnp.int32, (tile, tile), 0)
    for k in range(share):
        a = pl.program_id(0) * share + k
        moved = jnp.zeros((tile, lpc * tile), F32)
        for h in range(2):
            pick = (rows == order_ref[k, h : h + 1, :]).astype(BF16)
            moved = moved + dot(pick, recv_ref[slot_ref[h, a]], NN)
        for b in range(lpc):
            high, low = halves(fronts[b][k] + moved[:, b * tile : (b + 1) * tile])
            high_ref[k, b] = high
            low_ref[k, b] = low


def assemble_panel(fronts, order, slots, received):
    local_rows, tile, _ = fronts[0].shape
    lpc = len(fronts)
    share = 4 if local_rows % 4 == 0 else 1
    out = (local_rows, lpc, tile, tile)
    return pl.pallas_call(
        functools.partial(panel_kernel, lpc, share),
        out_shape=(jax.ShapeDtypeStruct(out, BF16), jax.ShapeDtypeStruct(out, BF16)),
        grid_spec=pltpu.PrefetchScalarGridSpec(
            num_scalar_prefetch=1,
            grid=(local_rows // share,),
            in_specs=[pl.BlockSpec((share, tile, tile), lambda a, s: (a, 0, 0))] * lpc
            + [
                pl.BlockSpec((share, 2, tile), lambda a, s: (a, 0, 0)),
                whole(received.shape),
            ],
            out_specs=[pl.BlockSpec((share,) + out[1:], lambda a, s: (a, 0, 0, 0))] * 2,
        ),
        compiler_params=pltpu.CompilerParams(vmem_limit_bytes=VMEM_LIMIT),
    )(slots, *fronts, order, received)


def lead_slots(row_count, col_count, lead_rows, lead_cols):
    return [
        (a, b)
        for a in range(lead_rows)
        for b in range(lead_cols)
        if col_count * b <= row_count * a + row_count - 1 and col_count * b < TILES
    ]


def unpack_kernel(row_count, col_count, slots, g_ref, *blocks):
    tile = g_ref.shape[-1]
    place = {ab: n for n, ab in enumerate(slots)}
    for i in range(TILES):
        for j in range(i + 1):
            n = place[i // row_count, j // col_count]
            t, u = i // PWT, j // PWT
            rows = pl.ds((i % PWT) * tile, tile)
            cols = pl.ds((j % PWT) * tile, tile)
            source = ((i % row_count) * col_count + j % col_count) * len(slots) + n
            blocks[t * (t + 1) // 2 + u][rows, cols] = g_ref[source]


def unpack_lead(gathered, row_count, col_count, slots):
    width = PWT * gathered.shape[-1]
    count = STEPS * (STEPS + 1) // 2
    return pl.pallas_call(
        functools.partial(unpack_kernel, row_count, col_count, slots),
        out_shape=[jax.ShapeDtypeStruct((width, width), F32)] * count,
        compiler_params=pltpu.CompilerParams(vmem_limit_bytes=VMEM_LIMIT),
    )(gathered)


def block_kernel(d_ref, l_ref, v_ref, vb_ref, work):
    width = d_ref.shape[0]
    tile = width // PWT
    row = lax.broadcasted_iota(jnp.int32, (tile, tile), 0)
    col = lax.broadcasted_iota(jnp.int32, (tile, tile), 1)
    work[...] = d_ref[...]
    l_ref[...] = jnp.zeros((width, width), F32)
    v_ref[...] = jnp.zeros((width, width), F32)
    for k in range(PWT):
        low, high = k * tile, (k + 1) * tile
        block = work[low:high, low:high]
        block = jnp.where(row >= col, block, block.T)
        upper, inverse = factor_tile(block)
        l_ref[low:high, low:high] = jnp.where(row <= col, upper, 0.0).T
        if k > 0:
            v_ref[low:high, 0:low] = dot3(inverse, v_ref[low:high, 0:low], NN)
        v_ref[low:high, low:high] = inverse
        if k < PWT - 1:
            below = dot3(work[high:width, low:high], inverse, NT)
            l_ref[high:width, low:high] = below
            work[high:width, high:width] -= dot3(below, below, NT)
            v_ref[high:width, 0:high] -= dot3(below, v_ref[low:high, 0:high], NN)
    vb_ref[...] = v_ref[...].astype(BF16)


def factor_block(diagonal):
    shape = diagonal.shape
    return pl.pallas_call(
        block_kernel,
        out_shape=(
            jax.ShapeDtypeStruct(shape, F32),
            jax.ShapeDtypeStruct(shape, F32),
            jax.ShapeDtypeStruct(shape, BF16),
        ),
        scratch_shapes=[pltpu.VMEM(shape, F32)],
        compiler_params=pltpu.CompilerParams(vmem_limit_bytes=VMEM_LIMIT),
        cost_estimate=pl.CostEstimate(flops=3 * 10**10, bytes_accessed=4 * 10**6, transcendentals=0),
    )(diagonal)


def advance_kernel(count, v_ref, *refs):
    below, trail = refs[:count], refs[count : count + count * (count + 1) // 2]
    rest = refs[count + len(trail) :]
    lower, lower_b, out = rest[:count], rest[count : 2 * count], rest[2 * count :]
    for t in range(count):
        lower[t][...] = dot3(below[t][...], v_ref[...], NT)
        lower_b[t][...] = lower[t][...].astype(BF16)
    for t in range(count):
        for u in range(t + 1):
            n = t * (t + 1) // 2 + u
            out[n][...] = trail[n][...] - dot3(lower[t][...], lower[u][...], NT)


def advance(inverse, below, trail):
    count = len(below)
    shape = inverse.shape
    kinds = [F32] * count + [BF16] * count + [F32] * len(trail)
    out = pl.pallas_call(
        functools.partial(advance_kernel, count),
        out_shape=[jax.ShapeDtypeStruct(shape, k) for k in kinds],
        compiler_params=pltpu.CompilerParams(vmem_limit_bytes=VMEM_LIMIT),
        cost_estimate=pl.CostEstimate(flops=3 * 10**9, bytes_accessed=10**7, transcendentals=0),
    )(inverse, *below, *trail)
    return out[:count], out[count : 2 * count], out[2 * count :]


def side_by_side(parts):
    return jnp.concatenate([p.reshape(-1, p.shape[-1]) for p in parts], axis=1)


def own_kernel(row_count, ids_ref, own_ref, l_ref, v_ref, out_ref):
    k = pl.program_id(0)
    tile = own_ref.shape[-1]
    width = PWT * tile
    index = (ids_ref[1] * pl.num_programs(0) + k) * row_count + ids_ref[0]

    @pl.when(index < TILES)
    def _():
        first = pl.multiple_of((index % PWT) * tile, tile)
        for s in range(STEPS):
            out_ref[0, :, s * width : (s + 1) * width] = l_ref[index // PWT, s, pl.ds(first, tile), :]

    @pl.when(index >= TILES)
    def _():
        solved = []
        for s in range(STEPS):
            rest = side_by_side([own_ref[s * PWT + j, 0] for j in range(PWT)])
            for q in range(s):
                rest = rest - dot3(solved[q], l_ref[s, q], NT)
            solved.append(dot3(rest, v_ref[s], NT))
            out_ref[0, :, s * width : (s + 1) * width] = solved[s]


def own_rows(ids, own, lower, inverse, row_count):
    tile = own.shape[-1]
    share = own.shape[1]
    return pl.pallas_call(
        functools.partial(own_kernel, row_count),
        out_shape=jax.ShapeDtypeStruct((share, tile, TILES * tile), F32),
        grid_spec=pltpu.PrefetchScalarGridSpec(
            num_scalar_prefetch=1,
            grid=(share,),
            in_specs=[
                pl.BlockSpec((TILES, 1, tile, tile), lambda k, s: (0, k, 0, 0)),
                whole(lower.shape),
                whole(inverse.shape),
            ],
            out_specs=pl.BlockSpec((1, tile, TILES * tile), lambda k, s: (k, 0, 0)),
        ),
        compiler_params=pltpu.CompilerParams(vmem_limit_bytes=VMEM_LIMIT),
    )(ids, own, lower, inverse)


def solve_kernel(first, n_parts, *refs):
    parts = refs[:n_parts]
    l_ref, v_ref, out_ref = refs[n_parts:]
    tile = parts[0].shape[-1]
    width = PWT * tile
    count = parts[0].shape[1]
    step = min(4, count)
    where = [(n, j) for n, ref in enumerate(parts) for j in range(ref.shape[0])]
    if first:
        out_ref[0 : first * tile, :] = jnp.zeros((first * tile, out_ref.shape[1]), BF16)

    @pl.loop(0, -(-count // step))
    def _(i):
        a = jnp.minimum(i * step, count - step)
        rows = pl.ds(pl.multiple_of((a + first) * tile, tile), step * tile)
        done = []
        for s in range(STEPS):
            pieces = [parts[n][j, pl.ds(a, step)] for n, j in where[s * PWT : (s + 1) * PWT]]
            rest = side_by_side(pieces)
            if s > 0:
                rest = rest.astype(F32)
                for q in range(s):
                    rest = rest - dot(done[q], l_ref[s * (s - 1) // 2 + q], NT)
                rest = rest.astype(BF16)
            done.append(dot(rest, v_ref[s], NT).astype(BF16))
            out_ref[rows, s * width : (s + 1) * width] = done[s]


def solve_rows(parts, first, lower, inverse):
    tile = parts[0].shape[-1]
    count = parts[0].shape[1]
    rows = (first + count) * tile
    return pl.pallas_call(
        functools.partial(solve_kernel, first, len(parts)),
        out_shape=jax.ShapeDtypeStruct((rows, TILES * tile), BF16),
        compiler_params=pltpu.CompilerParams(vmem_limit_bytes=VMEM_LIMIT),
        cost_estimate=pl.CostEstimate(
            flops=count * tile * (TILES * tile) ** 2 * 2,
            bytes_accessed=4 * rows * TILES * tile,
            transcendentals=0,
        ),
    )(*parts, lower, inverse)


def join_kernel(slot_ref, order_ref, recv_ref, front_ref, out_ref):
    g = pl.program_id(0)
    tile, local_cols = recv_ref.shape[1:3]
    share = out_ref.shape[0] // (tile * local_cols)
    out_ref[...] = front_ref[...]
    for k in range(share):
        a = g * share + k
        for h in range(2):
            slot = slot_ref[h, a]

            @pl.when(slot >= 0)
            def _(a=a, k=k, h=h, slot=slot):
                @pl.loop(0, tile, unroll=8)
                def _(t):
                    first = (k * tile + order_ref[h, a, t]) * local_cols
                    first = pl.multiple_of(first, local_cols)
                    out_ref[pl.ds(first, local_cols), :] += recv_ref[slot, t].astype(F32)


def join_children(slots, order, received, front, steps):
    rows = front.shape[0] // steps
    block = pl.BlockSpec((rows, front.shape[1]), lambda g, *_: (g, 0))
    return pl.pallas_call(
        join_kernel,
        out_shape=jax.ShapeDtypeStruct(front.shape, F32),
        grid_spec=pltpu.PrefetchScalarGridSpec(
            num_scalar_prefetch=2,
            grid=(steps,),
            in_specs=[whole(received.shape), block],
            out_specs=block,
        ),
        compiler_params=pltpu.CompilerParams(vmem_limit_bytes=VMEM_LIMIT),
        cost_estimate=pl.CostEstimate(flops=0, bytes_accessed=8 * front.size, transcendentals=0),
    )(slots, order, received, front)


def final_kernel(row_count, col_count, ids_ref, xr_ref, xc_ref, front_ref, out_ref):
    g = pl.program_id(0)
    tile = out_ref.shape[-1]
    share = xr_ref.shape[0] // tile
    local_cols = xc_ref.shape[0] // tile
    last = row_count * (g * share + share - 1) + ids_ref[0]
    pair = 2 if local_cols % 2 == 0 else 1
    for b in range(0, local_cols, pair):
        some = last >= jnp.maximum(col_count * b + ids_ref[1], TILES)

        @pl.when(some)
        def _(b=b):
            update = dot(xr_ref[...], xc_ref[b * tile : (b + pair) * tile, :], NT)
            for k in range(share):
                row_tile = row_count * (g * share + k) + ids_ref[0]
                for j in range(pair):
                    col_tile = col_count * (b + j) + ids_ref[1]
                    keep = (row_tile >= col_tile) & (col_tile >= TILES)
                    at = pl.ds(k * tile * local_cols + b + j, tile, stride=local_cols)
                    part = update[k * tile : (k + 1) * tile, j * tile : (j + 1) * tile]
                    out_ref[at, :] = jnp.where(keep, front_ref[at, :] - part, 0.0)

        @pl.when(jnp.logical_not(some))
        def _(b=b):
            for j in range(pair):
                out_ref[pl.ds(b + j, share * tile, stride=local_cols), :] = jnp.zeros(
                    (share * tile, tile), F32
                )


def final_update(ids, xr, xc, front, row_count, col_count):
    rows = front.shape[0] // col_count
    block = pl.BlockSpec((rows, front.shape[1]), lambda g, *_: (g, 0))
    return pl.pallas_call(
        functools.partial(final_kernel, row_count, col_count),
        out_shape=jax.ShapeDtypeStruct(front.shape, F32),
        grid_spec=pltpu.PrefetchScalarGridSpec(
            num_scalar_prefetch=1,
            grid=(col_count,),
            in_specs=[
                pl.BlockSpec((xr.shape[0] // col_count, xr.shape[1]), lambda g, *_: (g, 0)),
                whole(xc.shape),
                block,
            ],
            out_specs=block,
        ),
        compiler_params=pltpu.CompilerParams(vmem_limit_bytes=VMEM_LIMIT),
        cost_estimate=pl.CostEstimate(
            flops=xr.size * xc.shape[0], bytes_accessed=8 * front.size, transcendentals=0
        ),
    )(ids, xr, xc, front)


def column_rows(part, first, local_cols, row_count, col_count, col_dev):
    fold = col_count // row_count
    begin = TILES // col_count
    part = jnp.pad(part, ((0, 0), (first - fold * begin, 0), (0, 0), (0, 0)))
    split = part.reshape(part.shape[0], local_cols - begin, fold, part.shape[2], part.shape[3])
    picked = split[:, :, 0]
    for f in range(1, fold):
        picked = jnp.where(col_dev // row_count == f, split[:, :, f], picked)
    return picked


def from_owner_row(own, row_count, col_count, row_dev, col_dev):
    away = row_dev ^ (col_dev % row_count)
    stride = row_count // 2
    while stride:
        pairs = []
        for r in range(row_count):
            for c in range(col_count):
                if (r ^ (c % row_count)) % (2 * stride) == 0:
                    pairs.append((r * col_count + c, (r ^ stride) * col_count + c))
        arrived = lax.ppermute(own, ("row", "col"), pairs)
        own = jnp.where(away % (2 * stride) == stride, arrived, own)
        stride //= 2
    return own


def gather_columns(panel, b, first, col_count, col_dev, gate):
    rows = panel[first:, b]
    n = rows.shape[0]
    count = min(col_count, TILES - col_count * b)
    if b > 0:
        rows, gate = lax.optimization_barrier((rows, gate))
    if b > 0 and 2 * count == col_count:
        half = (n + 1) // 2
        sent = lax.ppermute(rows[n - half :], "col", [(c, c + count) for c in range(count)])
        both = lax.all_gather(jnp.where(col_dev < count, rows[:half], sent), "col")
        return jnp.concatenate([both[:count], both[count:, 2 * half - n :]], axis=1)
    return lax.all_gather(rows, "col")[:count]


def shards(front_matrix, children, child_map, row_order):
    row_count = lax.axis_size("row")
    col_count = lax.axis_size("col")
    row_dev = lax.axis_index("row")
    col_dev = lax.axis_index("col")
    local_rows = front_matrix.shape[0]
    tile = front_matrix.shape[2]
    local_cols = front_matrix.shape[3]
    lrc = children.shape[1]
    lead_cols = -(-TILES // col_count)
    lead_rows = -(-TILES // row_count)
    first = TILES // row_count
    share = local_rows // col_count
    front = front_matrix.reshape(local_rows * tile * local_cols, tile)
    ids = jnp.stack([row_dev, col_dev]).astype(jnp.int32)

    slots, orders = [], []
    for h in range(2):
        sources, targets, rank = slot_ranks(child_map[h], row_count)
        lands = (child_map[h] // row_count)[:, None] == jnp.arange(local_rows, dtype=jnp.int32)[None, :]
        lands = (lands & (targets == row_dev)[:, None]).astype(jnp.int32)
        slot = sources * (2 * CAP) + h * CAP + rank
        landed = jnp.sum(lands, axis=0)
        slots.append(jnp.where(landed > 0, jnp.sum(lands * slot[:, None], axis=0), -1))
        turned = jnp.sum(lands[:, :, None] * row_order[h][:, None, :], axis=0)
        orders.append(jnp.where((landed > 0)[:, None], turned, -1))
    slots = jnp.stack(slots)
    orders = jnp.stack(orders)

    def exchange(packed):
        arrived = lax.all_to_all(packed, "row", split_axis=0, concat_axis=0, tiled=True)
        return arrived.reshape((row_count * 2 * CAP,) + packed.shape[3:])

    kids = children.reshape(2, lrc, tile, local_cols, tile)
    near = kids[:, :, :, :lead_cols].reshape(2, lrc, tile, lead_cols * tile)
    near = exchange(pack_children(ids, child_map, near, row_count))
    far = pack_children(ids, child_map, kids, row_count)
    near, far = lax.optimization_barrier((near, far))
    fronts = [front_matrix[:, 0, :, b, 0, :] for b in range(lead_cols)]
    high, low = assemble_panel(fronts, orders.transpose(1, 0, 2), jnp.maximum(slots, 0), near)

    places = lead_slots(row_count, col_count, lead_rows, lead_cols)
    lead = jnp.stack([high[a, b].astype(F32) + low[a, b].astype(F32) for a, b in places]).astype(LINK)
    lead = lax.all_gather(lead, "col")
    parts = [gather_columns(high, b, first, col_count, col_dev, lead) for b in range(lead_cols)]
    lead = lax.all_gather(lead, "row")
    lead, far = lax.optimization_barrier((lead, far))
    far = exchange(far)
    blocks = unpack_lead(lead.reshape(-1, tile, tile).astype(F32), row_count, col_count, places)

    diagonals, inverses, inverses_b, lower, lower_b = [], [], [], {}, {}
    sent = []
    for s in range(STEPS):
        if s == STEPS - 1:
            picked = column_rows(parts[0], first, local_cols, row_count, col_count, col_dev)
            blocks[0], picked = lax.optimization_barrier((blocks[0], picked))
            sent.append(from_owner_row(picked, row_count, col_count, row_dev, col_dev))
        c, v, vb = factor_block(blocks[0])
        diagonals.append(c)
        inverses.append(v)
        inverses_b.append(vb)
        left = STEPS - 1 - s
        if left:
            index = lambda t, u: t * (t + 1) // 2 + u
            below = [blocks[index(t, 0)] for t in range(1, left + 1)]
            trail = [blocks[index(t, u)] for t in range(1, left + 1) for u in range(1, t + 1)]
            low_f, low_b, blocks = advance(v, below, trail)
            blocks = list(blocks)
            for n in range(left):
                lower[s + 1 + n, s] = low_f[n]
                lower_b[s + 1 + n, s] = low_b[n]
    inverse = jnp.stack(inverses)
    inverse_b = jnp.stack(inverses_b)
    lower_b = jnp.stack([lower_b[t, u] for t in range(1, STEPS) for u in range(t)])

    joined = join_children(slots, jnp.maximum(orders, 0), far, front, col_count)
    inverse_b, joined = lax.optimization_barrier((inverse_b, joined))
    for p in parts[1:]:
        picked = column_rows(p, first, local_cols, row_count, col_count, col_dev)
        sent.append(from_owner_row(picked, row_count, col_count, row_dev, col_dev))
    xr = solve_rows(parts, first, lower_b, inverse_b)
    xc = solve_rows(sent, TILES // col_count, lower_b, inverse_b)
    schur_part = final_update(ids, xr, xc, joined, row_count, col_count)

    low, parts = lax.optimization_barrier((low, parts))
    rest = low.reshape((col_count, share) + low.shape[1:])
    rest = lax.all_to_all(rest, "col", split_axis=0, concat_axis=0, tiled=True)
    mine = []
    for b, p in enumerate(parts):
        upper = jnp.stack(
            [
                lax.dynamic_index_in_dim(p, jnp.maximum(col_dev * share + k - first, 0), 1, False)
                for k in range(share)
            ],
            axis=1,
        )
        mine.append(upper.astype(F32) + rest[: p.shape[0], :, b].astype(F32))
    nothing = jnp.zeros_like(diagonals[0])
    square = jnp.stack(
        [
            diagonals[t] if t == u else lower[t, u] if u < t else nothing
            for t in range(STEPS)
            for u in range(STEPS)
        ]
    ).reshape((STEPS, STEPS) + nothing.shape)
    factor_part = own_rows(ids, jnp.concatenate(mine, axis=0), square, inverse, row_count)
    return (
        schur_part.reshape(front_matrix.shape),
        factor_part.reshape(share, 1, tile, TILES * tile),
    )


def solution(mesh):
    placed = (
        P(None, "row", None, None, "col", None),
        P(None, None, "row", None, None, "col", None),
        P(),
        P(),
    )
    return jax.shard_map(
        shards,
        mesh=mesh,
        in_specs=placed,
        out_specs=(P(None, "row", None, None, "col", None), P("col", "row", None, None)),
        check_vma=False,
    )
```

time: 2250 us -> 504 us (0.22)
  waiting for transfers between devices: 1020 us -> 65.9 us
  other arithmetic: 608 us -> 70 us
  local copies, waits for them, and re-layouts: 342 us -> 34.8 us
  matrix products: 234 us -> 0 us
  Pallas kernels: 0 us -> 224 us
  blocking collectives: 0 us -> 62.3 us
    psum x9 -> x0, waiting for transfers between devices: 999 us -> none  [from_root(): return lax.psum(kept, axis)]
    another operation x52 -> x7, other arithmetic: 357 us -> 8.03 us  [the longest x1 2.52 us: shards(): jnp.stack([lower_b[t, u] for t in range(1, STEPS) for u in range(t)])]
    pallas_call x0 -> x12, Pallas kernels: none -> 224 us  [the longest x2 58.2 us: factor_block(): pl.pallas_call(block_kernel, out_shape=(jax.ShapeDtypeStruct(shape, F32),...]
    dot_general x10 -> x0, matrix products: 158 us -> none  [the longest x1 87 us: shards(): jnp.einsum('atk,buk->atbu', stacked, stacked_cols, precision=lax.Precisio...]
    reshape x14 -> x2, local copies, waits for them, and re-layouts: 136 us -> 2.58 us  [the longest x1 1.45 us: shards(): rest = low.reshape((col_count, share) + low.shape[1:])]
    unnamed x1 -> x0, other arithmetic: 92.9 us -> none
    another operation x39 -> x0, matrix products: 76.4 us -> none  [the longest x21 70.8 us: shards(): jax.scipy.linalg.solve_triangular(cholesky_factor, flat_cols.T, lower=True)]
    unnamed x64 -> x42, local copies, waits for them, and re-layouts: 76.8 us -> 11.1 us
  transfers between devices with their start and end apart: 11 -> 10, of which waited for: 10 -> 2; matrix products, arithmetic and copies ran while one was open for 11% -> 18% of each run, Pallas kernels for 0% -> 31%
where the time goes in v1:
time: 504 us; the launch traced here: 495 us
  Pallas kernels  224 us (44%)
  other arithmetic  70 us (14%)
  waiting for transfers between devices  65.9 us (13%)
  blocking collectives  62.3 us (12%)
  local copies, waits for them, and re-layouts  34.8 us (7%)
  starting transfers between devices  24.1 us (5%)
  between operations  14.6 us (3%)
    pallas_call x2, Pallas kernels, factor_block(): pl.pallas_call(block_kernel, out_shape=(jax.ShapeDtypeStruct(shape, F32),...  58.2 us
    pallas_call x1, Pallas kernels, final_update(): pl.pallas_call(functools.partial(final_kernel, row_count, col_count), out...  44.6 us
    all_gather x1, waiting for transfers between devices, gather_columns(): both = lax.all_gather(jnp.where(col_dev < count, rows[:half], sent), 'col')  40.5 us
    pallas_call x2, Pallas kernels, solve_rows(): pl.pallas_call(functools.partial(solve_kernel, first, len(parts)), out_sh...  38 us
    all_gather x1, blocking collectives, shards(): lead = lax.all_gather(lead, 'col')  34.5 us
    pallas_call x1, Pallas kernels, join_children(): pl.pallas_call(join_kernel, out_shape=jax.ShapeDtypeStruct(front.shape, F...  29.6 us
    pallas_call x1, other arithmetic, factor_block(): pl.pallas_call(block_kernel, out_shape=(jax.ShapeDtypeStruct(shape, F32),...  29 us
    all_gather x1, blocking collectives, shards(): lead = lax.all_gather(lead, 'row')  27.8 us
  transfers between devices with their start and end apart: 10, of which 2 were waited for; matrix products, arithmetic and copies ran while one was open for 18% of the time, Pallas kernels for 31%

profile of v1, /device:TPU:24, one launch (start us, length us, event | category | flops | bytes accessed | tf_op | source)
XLA Modules:
  0.0 495.4 jit_solution(10143268465815303154)
XLA Ops:
  13.6 3.5 all-to-all-start
  17.3 7.6 %shard_map.60 = bf16[4,2,2,128,16,128]{5,4,3,2,1,0:T(8,128)(2,1)} custom-call(s32[2]{0:T(128)} %pad_add_fusion.2.ids_ref, s32[2,16]{1,0:T(2,128)} %map_ref.3, bf16[2,4,128,16,128]{4,3,2,1,0:T(8,128)(2,1)} %bitcast.151), custom_call_target="tpu_custom_call" | custom-call | tf_op jit(solution)/shard_map/pallas_call | solution.py:115
  27.8 4.7 fusion.26
  33.6 8.7 %shard_map.61 = (bf16[32,2,128,128]{3,2,1,0:T(8,128)(2,1)}, bf16[32,2,128,128]{3,2,1,0:T(8,128)(2,1)}) custom-call(s32[2,32]{1,0:T(2,128)} %get-tuple-element.133.slot_ref, f32[32,128,128]{2,1,0:T(8,128)} %bitcast.148, f32[32,128,128]{2,1,0:T(8,128)} %bitcast.147, s32[32,2,128]{2,1,0:T(2,128)} %copy.30.refs_2_, bf16[16,128,256]{2,1,0:T(8,128)(2,1)} %bitcast.152), custom_call_target="tpu_custom_call" | custom-call | tf_op jit(solution)/shard_map/pallas_call | solution.py:150
  45.9 34.5 %all-gather.11 = f16[8,4,128,128]{3,2,1,0:T(8,128)(2,1)S(1)} all-gather(f16[1,4,128,128]{3,2,1,0:T(8,128)(2,1)S(1)} %pad_maximum_fusion.5), channel_id=1, replica_groups=mesh['row'=4,'col'=8] {'col'}, dimensions={0}, use_global_device_ids=true | all-gather | bytes 1179648 | tf_op jit(solution)/shard_map/all_gather | solution.py:528
  81.7 27.8 %all-gather.12 = f16[32,4,128,128]{3,2,1,0:T(8,128)(2,1)} all-gather(f16[8,4,128,128]{3,2,1,0:T(8,128)(2,1)S(1)} %all-gather.11), channel_id=4, replica_groups=mesh['row'=4,'col'=8] {'row'}, dimensions={0}, use_global_device_ids=true | all-gather | bytes 5242880 | tf_op jit(solution)/shard_map/all_gather | solution.py:530
  109.5 5.6 %all-to-all-start.1 = ((bf16[4,2,2,128,16,128]{5,4,3,2,1,0:T(8,128)(2,1)}), bf16[4,2,2,128,16,128]{5,4,3,2,1,0:T(8,128)(2,1)}, u32[]{:S(2)}, u32[]{:S(2)}) async-start(bf16[4,2,2,128,16,128]{5,4,3,2,1,0:T(8,128)(2,1)} %shard_map.60), calls=%async_computation.1 | async-start | bytes 16777216 | tf_op jit(solution)/shard_map/all_to_all | solution.py:515
  115.4 6.6 %bitcast_convert_fusion.g_ref = f32[128,128,128]{2,1,0:T(8,128)} fusion(f16[4,8,4,128,128]{4,3,2,1,0:T(8,128)(2,1)} %bitcast.143), kind=kLoop, calls=%fused_computation | loop fusion | flops 2097152 | bytes 12582912 | tf_op jit(solution)/shard_map/convert_element_type | solution.py:533
  122.0 6.2 %shard_map.62 = (f32[512,512]{1,0:T(8,128)}, f32[512,512]{1,0:T(8,128)}, f32[512,512]{1,0:T(8,128)}, f32[512,512]{1,0:T(8,128)}, f32[512,512]{1,0:T(8,128)}, /*index=5*/f32[512,512]{1,0:T(8,128)}) custom-call(f32[128,128,128]{2,1,0:T(8,128)} %bitcast_convert_fusion.g_ref), custom_call_target="tpu_custom_call" | custom-call | tf_op jit(solution)/shard_map/pallas_call | solution.py:192
  129.0 28.9 %shard_map.63 = (f32[512,512]{1,0:T(8,128)}, f32[512,512]{1,0:T(8,128)}, bf16[512,512]{1,0:T(8,128)(2,1)}) custom-call(f32[512,512]{1,0:T(8,128)} %get-tuple-element.47.d_ref), custom_call_target="tpu_custom_call" | custom-call | flops 30000001024 | bytes 4000000 | tf_op jit(solution)/shard_map/pallas_call | solution.py:226
  157.9 8.1 %shard_map.64 = (f32[512,512]{1,0:T(8,128)}, f32[512,512]{1,0:T(8,128)}, bf16[512,512]{1,0:T(8,128)(2,1)}, bf16[512,512]{1,0:T(8,128)(2,1)}, f32[512,512]{1,0:T(...) custom-call(f32[512,512]{1,0:T(8,128)} %get-tuple-element.48.v_ref, f32[512,512]{1,0:T(8,128)} %get-tuple-element.49.refs_0_, ...), custom_call_target="tpu_custom_call" | custom-call | flops 3000000000 | bytes 10000000 | tf_op jit(solution)/shard_map/pallas_call | solution.py:256
  166.0 29.3 %shard_map.65 = (f32[512,512]{1,0:T(8,128)}, f32[512,512]{1,0:T(8,128)}, bf16[512,512]{1,0:T(8,128)(2,1)}) custom-call(f32[512,512]{1,0:T(8,128)} %get-tuple-element.56.d_ref), custom_call_target="tpu_custom_call" | custom-call | flops 30000001024 | bytes 4000000 | tf_op jit(solution)/shard_map/pallas_call | solution.py:226
  205.1 4.9 pad.8
  213.7 40.5 %all-gather.10.cloned.1.call-done = bf16[120,128,128]{2,1,0:T(8,128)(2,1)} async-done(((bf16[15,128,128]{2,1,0:T(8,128)(2,1)}), bf16[120,128,128]{2,1,0:T(8,128)(2,1)}) %all-gather.10.cloned.1.call-update) | async-done | bytes 3932176 | tf_op jit(solution)/shard_map/all_gather | solution.py:480
  263.2 25.3 %collective-permute-done.3 = bf16[4,15,128,128]{3,2,1,0:T(8,128)(2,1)} collective-permute-done((bf16[4,15,128,128]{3,2,1,0:T(8,128)(2,1)S(1)}, bf16[4,15,128,128]{3,2,1,0:T(8,128)(2,1)}, u32[]{:S(2)}, u32[]{:S(2)}) %collective-permute-start.3) | collective-permute-done | bytes 1966112 | tf_op jit(solution)/shard_map/ppermute | solution.py:465
  295.5 5.1 %all-to-all-start.2 = ((bf16[8,4,2,128,128]{4,3,1,2,0:T(8,128)(2,1)}), bf16[8,4,2,128,128]{4,3,1,2,0:T(8,128)(2,1)}, u32[]{:S(2)}, u32[]{:S(2)}) async-start(bf16[8,4,2,128,128]{4,3,1,2,0:T(8,128)(2,1)} %copy.35), calls=%async_computation.2 | async-start | bytes 4194304 | tf_op jit(solution)/shard_map/all_to_all | solution.py:571
  300.6 4.5 broadcast_select_fusion
  310.8 29.6 %shard_map.66.front_ref = f32[65536,128]{1,0:T(8,128)} custom-call(s32[2,32]{1,0:T(2,128)} %get-tuple-element.132.slot_ref, s32[2,32,128]{2,1,0:T(8,128)} %get-tuple-element.128.order_ref, bf16[16,128,16,128]{3,2,1,0:T(8,128)(2,1)} %bitcast.31.recv_ref, f32[65536,128]{1,0:T(8,128)} %bitcast.138), custom_call_target="tpu_custom_call" | custom-call | bytes 67108864 | tf_op jit(solution)/shard_map/pallas_call | solution.py:378
  342.0 29.0 %shard_map.71 = (f32[9,512,512]{2,1,0:T(8,128)}, bf16[512,512]{1,0:T(8,128)(2,1)S(1)}, f32[512,512]{1,0:T(8,128)}) fusion(f32[9,512,512]{2,1,0:T(8,128)} %get-tuple-element.93, f32[512,512]{1,0:T(8,128)} %get-tuple-element.64), kind=kCustom, calls=%fused_computation.21 | custom fusion | flops 30000001024 | bytes 3670016 | tf_op jit(solution)/shard_map/pallas_call | solution.py:226
  376.8 24.5 %shard_map.67.xr_ref = bf16[4096,1536]{1,0:T(8,128)(2,1)} custom-call(bf16[8,29,128,128]{3,2,1,0:T(8,128)(2,1)} %bitcast.146, bf16[4,29,128,128]{3,2,1,0:T(8,128)(2,1)} %copy-done.1, bf16[3,512,512]{2,1,0:T(8,128)(2,1)} %pad_maximum_fusion.3.refs_2_, bf16[3,512,512]{2,1,0:T(8,128)(2,1)} %pad_maximum_fusion.4.refs_3_), custom_call_target="tpu_custom_call" | custom-call | flops 17515413504 | bytes 25165824 | tf_op jit(solution)/shard_map/pallas_call | solution.py:344
  405.9 19.9 %shard_map.70 = f32[4,128,1536]{2,1,0:T(8,128)} custom-call(s32[2]{0:T(128)} %pad_add_fusion.2.ids_ref, f32[12,4,128,128]{3,2,1,0:T(8,128)} %pad_maximum_fusion.1.own_ref, f32[3,3,512,512]{3,2,1,0:T(8,128)} %bitcast.46.l_ref, f32[3,512,512]{2,1,0:T(8,128)} %pad_maximum_fusion.2.v_ref), custom_call_target="tpu_custom_call" | custom-call | tf_op jit(solution)/shard_map/pallas_call | solution.py:295
  425.8 4.4 broadcast_select_fusion.1.refs_0_
  430.2 13.5 %shard_map.68.xc_ref = bf16[2048,1536]{1,0:T(8,128)(2,1)} custom-call(bf16[8,15,128,128]{3,2,1,0:T(8,128)(2,1)} %broadcast_select_fusion.1.refs_0_, bf16[4,15,128,128]{3,2,1,0:T(8,128)(2,1)} %broadcast_select_fusion.3.refs_1_, bf16[3,512,512]{2,1,0:T(8,128)(2,1)} %pad_maximum_fusion.3.refs_2_, bf16[3,512,512]{2,1,0:T(8,128)(2,1)} %pad_maximum_fusion.4.refs_3_), custom_call_target="tpu_custom_call" | custom-call | flops 9059696640 | bytes 12582912 | tf_op jit(solution)/shard_map/pallas_call | solution.py:344
  443.7 44.6 %shard_map.69 = f32[65536,128]{1,0:T(8,128)} custom-call(s32[2]{0:T(128)} %pad_add_fusion.2.ids_ref, bf16[4096,1536]{1,0:T(8,128)(2,1)} %shard_map.67.xr_ref, bf16[2048,1536]{1,0:T(8,128)(2,1)} %shard_map.68.xc_ref, f32[65536,128]{1,0:T(8,128)} %shard_map.66.front_ref), custom_call_target="tpu_custom_call" | custom-call | flops 12884901888 | bytes 67108864 | tf_op jit(solution)/shard_map/pallas_call | solution.py:425
  (109 shorter events, 63.4 us)
Async XLA Ops:
  7.2 10.1 %copy-start.14 = (s32[2,16]{1,0:T(2,128)S(1)}, s32[2,16]{1,0:T(2,128)}, u32[]{:S(2)}) copy-start(s32[2,16]{1,0:T(2,128)} %map_ref.3) | copy-start | bytes 388
  13.6 18.9 %all-to-all-start = ((bf16[4,2,2,128,256]{4,3,2,1,0:T(8,128)(2,1)}), bf16[4,2,2,128,256]{4,3,2,1,0:T(8,128)(2,1)S(1)}, u32[]{:S(2)}, u32[]{:S(2)}) async-start(bf16[4,2,2,128,256]{4,3,2,1,0:T(8,128)(2,1)} %shard_map.59), calls=%async_computation | async-start | bytes 2097152 | tf_op jit(solution)/shard_map/all_to_all | solution.py:515
  17.2 188.0 %all-gather.8.cloned.1.call-start = ((), (), s32[]{:S(2)}) async-start(), calls=%async_computation.3 | async-start | bytes 8552448 | tf_op jit(solution)/shard_map/all_gather | solution.py:482
  17.3 8.2 %copy-start.15 = (s32[2,16,128]{2,1,0:T(8,128)S(1)}, s32[2,16,128]{2,1,0:T(8,128)}, u32[]{:S(2)}) copy-start(s32[2,16,128]{2,1,0:T(8,128)} %param.7) | copy-start | bytes 49156
  80.4 47.7 %collective-permute-start = (bf16[15,128,128]{2,1,0:T(8,128)(2,1)S(1)}, bf16[15,128,128]{2,1,0:T(8,128)(2,1)S(1)}, u32[]{:S(2)}, u32[]{:S(2)}) collective-permute-start(bf16[15,128,128]{2,1,0:T(8,128)(2,1)S(1)} %slice.101), channel_id=1, source_target_pairs={{0,4},{1,5},{2,6},{3,7},{8,12},{9,13},{10,14},{11,15},{16,20},{17,... | collective-permute-start | bytes 1474568 | tf_op jit(solution)/shard_map/ppermute | solution.py:479
  109.5 186.0 %all-to-all-start.1 = ((bf16[4,2,2,128,16,128]{5,4,3,2,1,0:T(8,128)(2,1)}), bf16[4,2,2,128,16,128]{5,4,3,2,1,0:T(8,128)(2,1)}, u32[]{:S(2)}, u32[]{:S(2)}) async-start(bf16[4,2,2,128,16,128]{5,4,3,2,1,0:T(8,128)(2,1)} %shard_map.60), calls=%async_computation.1 | async-start | bytes 16777216 | tf_op jit(solution)/shard_map/all_to_all | solution.py:515
  115.2 139.1 %all-gather.10.cloned.1.call-start = ((), (), s32[]{:S(2)}) async-start(), calls=%async_computation.4 | async-start | bytes 4423680 | tf_op jit(solution)/shard_map/all_gather | solution.py:480
  166.0 29.3 %copy-start.5 = (f32[512,512]{1,0:T(8,128)S(1)}, f32[512,512]{1,0:T(8,128)}, u32[]{:S(2)}) copy-start(f32[512,512]{1,0:T(8,128)} %get-tuple-element.73) | copy-start | bytes 3145732
  195.3 3.7 copy-start.7
  197.9 3.2 copy-start.4
  198.9 3.2 copy-start.9
  198.9 3.2 copy-start.16
  198.9 3.2 copy-start.17
  212.4 88.2 %collective-permute-start.1 = (bf16[8,15,128,128]{3,2,1,0:T(8,128)(2,1)}, bf16[8,15,128,128]{3,2,1,0:T(8,128)(2,1)}, u32[]{:S(2)}, u32[]{:S(2)}) collective-permute-start(bf16[8,15,128,128]{3,2,1,0:T(8,128)(2,1)} %fusion.1), channel_id=1, source_target_pairs={{0,16},{4,20},{9,25},{13,29},{18,2},{22,6},{27,11},{31,15}} | collective-permute-start | bytes 11796488 | tf_op jit(solution)/shard_map/ppermute | solution.py:465
  261.8 26.6 %collective-permute-start.3 = (bf16[4,15,128,128]{3,2,1,0:T(8,128)(2,1)S(1)}, bf16[4,15,128,128]{3,2,1,0:T(8,128)(2,1)}, u32[]{:S(2)}, u32[]{:S(2)}) collective-permute-start(bf16[4,15,128,128]{3,2,1,0:T(8,128)(2,1)S(1)} %fusion.3), channel_id=1, source_target_pairs={{0,16},{4,20},{9,25},{13,29},{18,2},{22,6},{27,11},{31,15}} | collective-permute-start | bytes 5898248 | tf_op jit(solution)/shard_map/ppermute | solution.py:465
  263.2 30.9 %copy-start.3 = (bf16[32,2,128,128]{3,2,1,0:T(8,128)(2,1)S(1)}, bf16[32,2,128,128]{3,2,1,0:T(8,128)(2,1)}, u32[]{:S(2)}) copy-start(bf16[32,2,128,128]{3,2,1,0:T(8,128)(2,1)} %get-tuple-element.71) | copy-start | bytes 6291460
  291.5 49.0 %collective-permute-start.4 = (bf16[4,15,128,128]{3,2,1,0:T(8,128)(2,1)S(1)}, bf16[4,15,128,128]{3,2,1,0:T(8,128)(2,1)}, u32[]{:S(2)}, u32[]{:S(2)}) collective-permute-start(bf16[4,15,128,128]{3,2,1,0:T(8,128)(2,1)S(1)} %broadcast_select_fusion.2), channel_id=1, source_target_pairs={{0,8},{2,10},{4,12},{6,14},{9,1},{11,3},{13,5},{15,7},{16,24},{18,... | collective-permute-start | bytes 5898248 | tf_op jit(solution)/shard_map/ppermute | solution.py:465
  295.5 105.7 %all-to-all-start.2 = ((bf16[8,4,2,128,128]{4,3,1,2,0:T(8,128)(2,1)}), bf16[8,4,2,128,128]{4,3,1,2,0:T(8,128)(2,1)}, u32[]{:S(2)}, u32[]{:S(2)}) async-start(bf16[8,4,2,128,128]{4,3,1,2,0:T(8,128)(2,1)} %copy.35), calls=%async_computation.2 | async-start | bytes 4194304 | tf_op jit(solution)/shard_map/all_to_all | solution.py:571
  300.6 7.6 %copy-start.13 = (bf16[512,512]{1,0:T(8,128)(2,1)S(1)}, bf16[512,512]{1,0:T(8,128)(2,1)}, u32[]{:S(2)}) copy-start(bf16[512,512]{1,0:T(8,128)(2,1)} %get-tuple-element.54) | copy-start | bytes 1572868
  305.1 120.6 %collective-permute-start.2 = (bf16[8,15,128,128]{3,2,1,0:T(8,128)(2,1)}, bf16[8,15,128,128]{3,2,1,0:T(8,128)(2,1)}, u32[]{:S(2)}, u32[]{:S(2)}) collective-permute-start(bf16[8,15,128,128]{3,2,1,0:T(8,128)(2,1)} %broadcast_select_fusion), channel_id=1, source_target_pairs={{0,8},{2,10},{4,12},{6,14},{9,1},{11,3},{13,5},{15,7},{16,24},{18,... | collective-permute-start | bytes 11796488 | tf_op jit(solution)/shard_map/ppermute | solution.py:465
  342.0 29.0 %copy-start.11 = (bf16[512,512]{1,0:T(8,128)(2,1)S(1)}, bf16[512,512]{1,0:T(8,128)(2,1)}, u32[]{:S(2)}) copy-start(bf16[512,512]{1,0:T(8,128)(2,1)} %get-tuple-element.61) | copy-start | bytes 1572868
  342.0 29.0 %copy-start.12 = (bf16[512,512]{1,0:T(8,128)(2,1)S(1)}, bf16[512,512]{1,0:T(8,128)(2,1)}, u32[]{:S(2)}) copy-start(bf16[512,512]{1,0:T(8,128)(2,1)} %get-tuple-element.62) | copy-start | bytes 1572868
  371.0 3.8 copy-start.8
  371.0 3.8 copy-start.10
  (4 other events, 7.4 us)
Sparse Core Ops, SparseCore 0:
  45.0 138.3 all-gather.7
  185.6 68.5 all-gather.9

commit v2 on v1

--- a/solution.py
+++ b/solution.py
@@ -69,6 +69,8 @@
         square = {(a, b): spread_row(columns[b], a) for a in range(8) for b in range(a + 1)}
         lrow = [spread_row(left[s], i) for i in range(8)]
         rrow = [spread_row(right[s], i) for i in range(8)]
+        more = s + 1 < groups
+        ahead = [spread_lane(left[s + 1], 8 * s + b) for b in range(8)] if more else None
         new_left = jnp.zeros((8, size), F32)
         new_right = jnp.zeros((8, size), F32)
         for i in range(8):
@@ -76,21 +78,27 @@
             below = {a: square[a, i] * inverse for a in range(i + 1, 8)}
             lrow[i] = lrow[i] * inverse
             rrow[i] = rrow[i] * inverse
+            if more:
+                ahead[i] = ahead[i] * inverse
             for a in range(i + 1, 8):
                 for b in range(i + 1, a + 1):
                     square[a, b] = square[a, b] - below[a] * below[b]
                 lrow[a] = lrow[a] - below[a] * lrow[i]
                 rrow[a] = rrow[a] - below[a] * rrow[i]
+                if more:
+                    ahead[a] = ahead[a] - below[a] * ahead[i]
             new_left = jnp.where(sub == i, lrow[i], new_left)
             new_right = jnp.where(sub == i, rrow[i], new_right)
         left[s], right[s] = new_left, new_right
-        if s < groups - 1:
-            turned = new_left.T
-            for t in range(s + 1, groups):
-                for a in range(8):
-                    scale = jnp.broadcast_to(turned[8 * t : 8 * t + 8, a : a + 1], (8, size))
-                    left[t] = left[t] - scale * lrow[a]
-                    right[t] = right[t] - scale * rrow[a]
+        if more:
+            for a in range(8):
+                left[s + 1] = left[s + 1] - ahead[a] * lrow[a]
+                right[s + 1] = right[s + 1] - ahead[a] * rrow[a]
+        if s + 2 < groups:
+            both = dot3(new_left, jnp.concatenate([new_left, new_right], 1), TN)
+            for t in range(s + 2, groups):
+                left[t] = left[t] - both[8 * t : 8 * t + 8, :size]
+                right[t] = right[t] - both[8 * t : 8 * t + 8, size:]
     return jnp.concatenate(left, 0), jnp.concatenate(right, 0)
 
 
@@ -266,59 +274,58 @@
     return jnp.concatenate([p.reshape(-1, p.shape[-1]) for p in parts], axis=1)
 
 
-def own_kernel(row_count, ids_ref, own_ref, l_ref, v_ref, out_ref):
-    k = pl.program_id(0)
-    tile = own_ref.shape[-1]
+def own_kernel(row_count, ids_ref, own_ref, *refs):
+    lower, inverse, out_ref = refs[: STEPS * (STEPS + 1) // 2], refs[-1 - STEPS : -1], refs[-1]
+    share, tile = own_ref.shape[1:3]
     width = PWT * tile
-    index = (ids_ref[1] * pl.num_programs(0) + k) * row_count + ids_ref[0]
-
-    @pl.when(index < TILES)
-    def _():
-        first = pl.multiple_of((index % PWT) * tile, tile)
-        for s in range(STEPS):
-            out_ref[0, :, s * width : (s + 1) * width] = l_ref[index // PWT, s, pl.ds(first, tile), :]
-
-    @pl.when(index >= TILES)
-    def _():
-        solved = []
-        for s in range(STEPS):
-            rest = side_by_side([own_ref[s * PWT + j, 0] for j in range(PWT)])
-            for q in range(s):
-                rest = rest - dot3(solved[q], l_ref[s, q], NT)
-            solved.append(dot3(rest, v_ref[s], NT))
-            out_ref[0, :, s * width : (s + 1) * width] = solved[s]
+    solved = []
+    for s in range(STEPS):
+        rest = side_by_side([own_ref[s * PWT + j] for j in range(PWT)])
+        for q in range(s):
+            rest = rest - dot3(solved[q], lower[s * (s + 1) // 2 + q][...], NT)
+        solved.append(dot3(rest, inverse[s][...], NT))
+        out_ref[:, s * width : (s + 1) * width] = solved[s]
+    for k in range(share):
+        index = (ids_ref[1] * share + k) * row_count + ids_ref[0]
+        for t in range(STEPS):
+
+            @pl.when(index // PWT == t)
+            def _(k=k, t=t, index=index):
+                source = pl.ds(pl.multiple_of((index % PWT) * tile, tile), tile)
+                target = pl.ds(k * tile, tile)
+                for s in range(STEPS):
+                    if s <= t:
+                        value = lower[t * (t + 1) // 2 + s][source, :]
+                    else:
+                        value = jnp.zeros((tile, width), F32)
+                    out_ref[target, s * width : (s + 1) * width] = value
 
 
 def own_rows(ids, own, lower, inverse, row_count):
-    tile = own.shape[-1]
-    share = own.shape[1]
+    share, tile = own.shape[1:3]
+    out = (share * tile, TILES * tile)
     return pl.pallas_call(
         functools.partial(own_kernel, row_count),
-        out_shape=jax.ShapeDtypeStruct((share, tile, TILES * tile), F32),
+        out_shape=jax.ShapeDtypeStruct(out, F32),
         grid_spec=pltpu.PrefetchScalarGridSpec(
             num_scalar_prefetch=1,
-            grid=(share,),
-            in_specs=[
-                pl.BlockSpec((TILES, 1, tile, tile), lambda k, s: (0, k, 0, 0)),
-                whole(lower.shape),
-                whole(inverse.shape),
-            ],
-            out_specs=pl.BlockSpec((1, tile, TILES * tile), lambda k, s: (k, 0, 0)),
+            grid=(1,),
+            in_specs=[whole(x.shape) for x in (own, *lower, *inverse)],
+            out_specs=whole(out),
         ),
         compiler_params=pltpu.CompilerParams(vmem_limit_bytes=VMEM_LIMIT),
-    )(ids, own, lower, inverse)
-
-
-def solve_kernel(first, n_parts, *refs):
-    parts = refs[:n_parts]
-    l_ref, v_ref, out_ref = refs[n_parts:]
+        cost_estimate=pl.CostEstimate(flops=6 * 10**9, bytes_accessed=15 * 10**6, transcendentals=0),
+    )(ids, own, *lower, *inverse)
+
+
+def solve_into(parts, lower, inverse, target, first):
     tile = parts[0].shape[-1]
     width = PWT * tile
     count = parts[0].shape[1]
     step = min(4, count)
     where = [(n, j) for n, ref in enumerate(parts) for j in range(ref.shape[0])]
     if first:
-        out_ref[0 : first * tile, :] = jnp.zeros((first * tile, out_ref.shape[1]), BF16)
+        target[0 : first * tile, :] = jnp.zeros((first * tile, target.shape[1]), BF16)
 
     @pl.loop(0, -(-count // step))
     def _(i):
@@ -326,15 +333,22 @@
         rows = pl.ds(pl.multiple_of((a + first) * tile, tile), step * tile)
         done = []
         for s in range(STEPS):
-            pieces = [parts[n][j, pl.ds(a, step)] for n, j in where[s * PWT : (s + 1) * PWT]]
-            rest = side_by_side(pieces)
+            rest = side_by_side([parts[n][j, pl.ds(a, step)] for n, j in where[s * PWT : (s + 1) * PWT]])
             if s > 0:
                 rest = rest.astype(F32)
                 for q in range(s):
-                    rest = rest - dot(done[q], l_ref[s * (s - 1) // 2 + q], NT)
+                    rest = rest - dot(done[q], lower[s * (s - 1) // 2 + q][...], NT)
                 rest = rest.astype(BF16)
-            done.append(dot(rest, v_ref[s], NT).astype(BF16))
-            out_ref[rows, s * width : (s + 1) * width] = done[s]
+            done.append(dot(rest, inverse[s][...], NT).astype(BF16))
+            target[rows, s * width : (s + 1) * width] = done[s]
+
+
+BELOW = STEPS * (STEPS - 1) // 2
+
+
+def solve_kernel(first, n_parts, *refs):
+    parts, blocks, out_ref = refs[:n_parts], refs[n_parts:-1], refs[-1]
+    solve_into(parts, blocks[:BELOW], blocks[BELOW:], out_ref, first)
 
 
 def solve_rows(parts, first, lower, inverse):
@@ -350,13 +364,21 @@
             bytes_accessed=4 * rows * TILES * tile,
             transcendentals=0,
         ),
-    )(*parts, lower, inverse)
-
-
-def join_kernel(slot_ref, order_ref, recv_ref, front_ref, out_ref):
+    )(*parts, *lower, *inverse)
+
+
+def final_kernel(row_count, col_count, n_parts, ids_ref, slot_ref, order_ref, *refs):
+    parts, blocks = refs[:n_parts], refs[n_parts : n_parts + BELOW + STEPS]
+    recv_ref, xr_ref, front_ref, out_ref, xc_ref = refs[n_parts + BELOW + STEPS :]
     g = pl.program_id(0)
-    tile, local_cols = recv_ref.shape[1:3]
-    share = out_ref.shape[0] // (tile * local_cols)
+    tile = out_ref.shape[-1]
+    share = xr_ref.shape[0] // tile
+    local_cols = xc_ref.shape[0] // tile
+
+    @pl.when(g == 0)
+    def _():
+        solve_into(parts, blocks[:BELOW], blocks[BELOW:], xc_ref, local_cols - parts[0].shape[1])
+
     out_ref[...] = front_ref[...]
     for k in range(share):
         a = g * share + k
@@ -367,33 +389,10 @@
             def _(a=a, k=k, h=h, slot=slot):
                 @pl.loop(0, tile, unroll=8)
                 def _(t):
-                    first = (k * tile + order_ref[h, a, t]) * local_cols
-                    first = pl.multiple_of(first, local_cols)
-                    out_ref[pl.ds(first, local_cols), :] += recv_ref[slot, t].astype(F32)
-
-
-def join_children(slots, order, received, front, steps):
-    rows = front.shape[0] // steps
-    block = pl.BlockSpec((rows, front.shape[1]), lambda g, *_: (g, 0))
-    return pl.pallas_call(
-        join_kernel,
-        out_shape=jax.ShapeDtypeStruct(front.shape, F32),
-        grid_spec=pltpu.PrefetchScalarGridSpec(
-            num_scalar_prefetch=2,
-            grid=(steps,),
-            in_specs=[whole(received.shape), block],
-            out_specs=block,
-        ),
-        compiler_params=pltpu.CompilerParams(vmem_limit_bytes=VMEM_LIMIT),
-        cost_estimate=pl.CostEstimate(flops=0, bytes_accessed=8 * front.size, transcendentals=0),
-    )(slots, order, received, front)
-
-
-def final_kernel(row_count, col_count, ids_ref, xr_ref, xc_ref, front_ref, out_ref):
-    g = pl.program_id(0)
-    tile = out_ref.shape[-1]
-    share = xr_ref.shape[0] // tile
-    local_cols = xc_ref.shape[0] // tile
+                    at = (k * tile + order_ref[h, a, t]) * local_cols
+                    at = pl.ds(pl.multiple_of(at, local_cols), local_cols)
+                    out_ref[at, :] += recv_ref[slot, t].astype(F32)
+
     last = row_count * (g * share + share - 1) + ids_ref[0]
     pair = 2 if local_cols % 2 == 0 else 1
     for b in range(0, local_cols, pair):
@@ -409,7 +408,7 @@
                     keep = (row_tile >= col_tile) & (col_tile >= TILES)
                     at = pl.ds(k * tile * local_cols + b + j, tile, stride=local_cols)
                     part = update[k * tile : (k + 1) * tile, j * tile : (j + 1) * tile]
-                    out_ref[at, :] = jnp.where(keep, front_ref[at, :] - part, 0.0)
+                    out_ref[at, :] = jnp.where(keep, out_ref[at, :] - part, 0.0)
 
         @pl.when(jnp.logical_not(some))
         def _(b=b):
@@ -419,27 +418,26 @@
                 )
 
 
-def final_update(ids, xr, xc, front, row_count, col_count):
+def final_update(ids, slots, order, parts, lower, inverse, received, xr, front, row_count, col_count):
     rows = front.shape[0] // col_count
     block = pl.BlockSpec((rows, front.shape[1]), lambda g, *_: (g, 0))
+    held = (*parts, *lower, *inverse, received)
     return pl.pallas_call(
-        functools.partial(final_kernel, row_count, col_count),
+        functools.partial(final_kernel, row_count, col_count, len(parts)),
         out_shape=jax.ShapeDtypeStruct(front.shape, F32),
         grid_spec=pltpu.PrefetchScalarGridSpec(
-            num_scalar_prefetch=1,
+            num_scalar_prefetch=3,
             grid=(col_count,),
-            in_specs=[
-                pl.BlockSpec((xr.shape[0] // col_count, xr.shape[1]), lambda g, *_: (g, 0)),
-                whole(xc.shape),
-                block,
-            ],
+            in_specs=[whole(x.shape) for x in held]
+            + [pl.BlockSpec((xr.shape[0] // col_count, xr.shape[1]), lambda g, *_: (g, 0)), block],
             out_specs=block,
+            scratch_shapes=[pltpu.VMEM((received.shape[2] * front.shape[1], xr.shape[1]), BF16)],
         ),
         compiler_params=pltpu.CompilerParams(vmem_limit_bytes=VMEM_LIMIT),
         cost_estimate=pl.CostEstimate(
-            flops=xr.size * xc.shape[0], bytes_accessed=8 * front.size, transcendentals=0
+            flops=2 * xr.size * xr.shape[1], bytes_accessed=8 * front.size, transcendentals=0
         ),
-    )(ids, xr, xc, front)
+    )(ids, slots, order, *held, xr, front)
 
 
 def column_rows(part, first, local_cols, row_count, col_count, col_dev):
@@ -468,18 +466,23 @@
     return own
 
 
-def gather_columns(panel, b, first, col_count, col_dev, gate):
+def gather_columns(panel, b, first, col_count, col_dev):
     rows = panel[first:, b]
     n = rows.shape[0]
     count = min(col_count, TILES - col_count * b)
-    if b > 0:
-        rows, gate = lax.optimization_barrier((rows, gate))
     if b > 0 and 2 * count == col_count:
         half = (n + 1) // 2
         sent = lax.ppermute(rows[n - half :], "col", [(c, c + count) for c in range(count)])
-        both = lax.all_gather(jnp.where(col_dev < count, rows[:half], sent), "col")
-        return jnp.concatenate([both[:count], both[count:, 2 * half - n :]], axis=1)
-    return lax.all_gather(rows, "col")[:count]
+        rows = jnp.where(col_dev < count, rows[:half], sent)
+    return lax.all_gather(rows, "col")
+
+
+def merge_columns(gathered, b, n, col_count):
+    count = min(col_count, TILES - col_count * b)
+    half = gathered.shape[1]
+    if half < n:
+        return jnp.concatenate([gathered[:count], gathered[count:, 2 * half - n :]], axis=1)
+    return gathered[:count]
 
 
 def shards(front_matrix, children, child_map, row_order):
@@ -526,7 +529,8 @@
     places = lead_slots(row_count, col_count, lead_rows, lead_cols)
     lead = jnp.stack([high[a, b].astype(F32) + low[a, b].astype(F32) for a, b in places]).astype(LINK)
     lead = lax.all_gather(lead, "col")
-    parts = [gather_columns(high, b, first, col_count, col_dev, lead) for b in range(lead_cols)]
+    height = local_rows - first
+    parts = [merge_columns(gather_columns(high, 0, first, col_count, col_dev), 0, height, col_count)]
     lead = lax.all_gather(lead, "row")
     lead, far = lax.optimization_barrier((lead, far))
     far = exchange(far)
@@ -537,12 +541,15 @@
     for s in range(STEPS):
         if s == STEPS - 1:
             picked = column_rows(parts[0], first, local_cols, row_count, col_count, col_dev)
-            blocks[0], picked = lax.optimization_barrier((blocks[0], picked))
+            blocks[0], picked, far = lax.optimization_barrier((blocks[0], picked, far))
             sent.append(from_owner_row(picked, row_count, col_count, row_dev, col_dev))
         c, v, vb = factor_block(blocks[0])
         diagonals.append(c)
         inverses.append(v)
         inverses_b.append(vb)
+        if s == 0 and lead_cols > 1:
+            later, _ = lax.optimization_barrier((high, vb))
+            late = gather_columns(later, lead_cols - 1, first, col_count, col_dev)
         left = STEPS - 1 - s
         if left:
             index = lambda t, u: t * (t + 1) // 2 + u
@@ -553,18 +560,21 @@
             for n in range(left):
                 lower[s + 1 + n, s] = low_f[n]
                 lower_b[s + 1 + n, s] = low_b[n]
-    inverse = jnp.stack(inverses)
-    inverse_b = jnp.stack(inverses_b)
-    lower_b = jnp.stack([lower_b[t, u] for t in range(1, STEPS) for u in range(t)])
-
-    joined = join_children(slots, jnp.maximum(orders, 0), far, front, col_count)
-    inverse_b, joined = lax.optimization_barrier((inverse_b, joined))
-    for p in parts[1:]:
-        picked = column_rows(p, first, local_cols, row_count, col_count, col_dev)
+    triangle = [
+        diagonals[t] if t == u else lower[t, u] for t in range(STEPS) for u in range(t + 1)
+    ]
+    below_b = [lower_b[t, u] for t in range(1, STEPS) for u in range(t)]
+
+    if lead_cols > 1:
+        late, inverses_b[-1] = lax.optimization_barrier((late, inverses_b[-1]))
+        parts.append(merge_columns(late, lead_cols - 1, height, col_count))
+        picked = column_rows(parts[-1], first, local_cols, row_count, col_count, col_dev)
+        inverses_b[-1], picked = lax.optimization_barrier((inverses_b[-1], picked))
         sent.append(from_owner_row(picked, row_count, col_count, row_dev, col_dev))
-    xr = solve_rows(parts, first, lower_b, inverse_b)
-    xc = solve_rows(sent, TILES // col_count, lower_b, inverse_b)
-    schur_part = final_update(ids, xr, xc, joined, row_count, col_count)
+    xr = solve_rows(parts, first, below_b, inverses_b)
+    schur_part = final_update(
+        ids, slots, jnp.maximum(orders, 0), sent, below_b, inverses_b, far, xr, front, row_count, col_count
+    )
 
     low, parts = lax.optimization_barrier((low, parts))
     rest = low.reshape((col_count, share) + low.shape[1:])
@@ -579,15 +589,8 @@
             axis=1,
         )
         mine.append(upper.astype(F32) + rest[: p.shape[0], :, b].astype(F32))
-    nothing = jnp.zeros_like(diagonals[0])
-    square = jnp.stack(
-        [
-            diagonals[t] if t == u else lower[t, u] if u < t else nothing
-            for t in range(STEPS)
-            for u in range(STEPS)
-        ]
-    ).reshape((STEPS, STEPS) + nothing.shape)
-    factor_part = own_rows(ids, jnp.concatenate(mine, axis=0), square, inverse, row_count)
+    factor_part = own_rows(ids, jnp.concatenate(mine, axis=0), triangle, inverses, row_count)
+
     return (
         schur_part.reshape(front_matrix.shape),
         factor_part.reshape(share, 1, tile, TILES * tile),

time: 504 us -> 431 us (0.86)
  other arithmetic: 70 us -> 33.6 us
  Pallas kernels: 224 us -> 206 us
  waiting for transfers between devices: 65.9 us -> 54.9 us
  local copies, waits for them, and re-layouts: 34.8 us -> 26 us
    all_gather x2, waiting for transfers between devices: 40.5 us -> 1.3 us  [gather_columns(): return lax.all_gather(rows, 'col')]
    ppermute x1, waiting for transfers between devices: 0.01 us -> 36.5 us  [gather_columns(): lax.ppermute(rows[n - half:], 'col', [(c, c + count) for c in range(count)])]
    pallas_call x2 -> x0, other arithmetic: 32 us -> none  [the longest x1 29 us: factor_block(): pl.pallas_call(block_kernel, out_shape=(jax.ShapeDtypeStruct(shape, F32),...]
    pallas_call x2 -> x1, Pallas kernels: 38 us -> 24.5 us  [solve_rows(): pl.pallas_call(functools.partial(solve_kernel, first, len(parts)), out_sh...]
    pallas_call x2 -> x1, Pallas kernels: 74.2 us -> 62.5 us  [final_update(): pl.pallas_call(functools.partial(final_kernel, row_count, col_count, len(...]
    pallas_call x2 -> x3, Pallas kernels: 58.2 us -> 68.1 us  [factor_block(): pl.pallas_call(block_kernel, out_shape=(jax.ShapeDtypeStruct(shape, F32),...]
    unnamed x42 -> x12, local copies, waits for them, and re-layouts: 11.1 us -> 2.27 us
    ppermute x4, waiting for transfers between devices: 25.3 us -> 17 us  [from_owner_row(): arrived = lax.ppermute(own, ('row', 'col'), pairs)]
  transfers between devices with their start and end apart: 10 -> 10, of which waited for: 2 -> 4; matrix products, arithmetic and copies ran while one was open for 18% -> 11% of each run, Pallas kernels for 31% -> 31%
where the time goes in v2:
time: 431 us; the launch traced here: 425 us
  Pallas kernels  206 us (48%)
  blocking collectives  62.3 us (14%)
  waiting for transfers between devices  54.9 us (13%)
  other arithmetic  33.6 us (8%)
  starting transfers between devices  28.5 us (7%)
  local copies, waits for them, and re-layouts  26 us (6%)
  between operations  14.6 us (3%)
    pallas_call x3, Pallas kernels, factor_block(): pl.pallas_call(block_kernel, out_shape=(jax.ShapeDtypeStruct(shape, F32),...  68.1 us
    pallas_call x1, Pallas kernels, final_update(): pl.pallas_call(functools.partial(final_kernel, row_count, col_count, len(...  62.5 us
    ppermute x1, waiting for transfers between devices, gather_columns(): lax.ppermute(rows[n - half:], 'col', [(c, c + count) for c in range(count)])  36.5 us
    all_gather x1, blocking collectives, shards(): lead = lax.all_gather(lead, 'col')  34.5 us
    all_gather x1, blocking collectives, shards(): lead = lax.all_gather(lead, 'row')  27.8 us
    pallas_call x1, Pallas kernels, solve_rows(): pl.pallas_call(functools.partial(solve_kernel, first, len(parts)), out_sh...  24.5 us
    ppermute x4, waiting for transfers between devices, from_owner_row(): arrived = lax.ppermute(own, ('row', 'col'), pairs)  17 us
    select_n x4, other arithmetic, from_owner_row(): own = jnp.where(away % (2 * stride) == stride, arrived, own)  15 us
  transfers between devices with their start and end apart: 10, of which 4 were waited for; matrix products, arithmetic and copies ran while one was open for 11% of the time, Pallas kernels for 31%

profile of v2, /device:TPU:24, one launch (start us, length us, event | category | flops | bytes accessed | tf_op | source)
XLA Modules:
  0.0 425.5 jit_solution(16434958915088555480)
XLA Ops:
  13.6 3.5 all-to-all-start
  17.3 7.6 %shard_map.60 = bf16[4,2,2,128,16,128]{5,4,3,2,1,0:T(8,128)(2,1)} custom-call(s32[2]{0:T(128)} %pad_add_fusion.2.ids_ref, s32[2,16]{1,0:T(2,128)} %map_ref.3, bf16[2,4,128,16,128]{4,3,2,1,0:T(8,128)(2,1)} %bitcast.124), custom_call_target="tpu_custom_call" | custom-call | tf_op jit(solution)/shard_map/pallas_call | solution.py:123
  27.7 4.7 %fusion.19 = (f32[32,1,128,1,1,128]{5,4,3,2,1,0:T(1,128)}, f32[32,1,128,1,1,128]{5,4,3,2,1,0:T(1,128)}) fusion(f32[32,1,128,16,1,128]{5,4,3,2,1,0:T(1,128)} %param.4), kind=kLoop, calls=%fused_computation.95 | loop fusion | bytes 8388608 | tf_op jit(solution)/shard_map/slice | solution.py:526
  33.4 8.7 %shard_map.61 = (bf16[32,2,128,128]{3,2,1,0:T(8,128)(2,1)}, bf16[32,2,128,128]{3,2,1,0:T(8,128)(2,1)}) custom-call(s32[2,32]{1,0:T(2,128)} %get-tuple-element.124.slot_ref, f32[32,128,128]{2,1,0:T(8,128)} %bitcast.122, f32[32,128,128]{2,1,0:T(8,128)} %bitcast.121, s32[32,2,128]{2,1,0:T(2,128)} %copy.32.refs_2_, bf16[16,128,256]{2,1,0:T(8,128)(2,1)} %bitcast.125), custom_call_target="tpu_custom_call" | custom-call | tf_op jit(solution)/shard_map/pallas_call | solution.py:158
  45.5 34.5 %all-gather.11 = f16[8,4,128,128]{3,2,1,0:T(8,128)(2,1)S(1)} all-gather(f16[1,4,128,128]{3,2,1,0:T(8,128)(2,1)S(1)} %pad_maximum_fusion.2), channel_id=1, replica_groups=mesh['row'=4,'col'=8] {'col'}, dimensions={0}, use_global_device_ids=true | all-gather | bytes 1179648 | tf_op jit(solution)/shard_map/all_gather | solution.py:531
  79.9 27.8 %all-gather.12 = f16[32,4,128,128]{3,2,1,0:T(8,128)(2,1)} all-gather(f16[8,4,128,128]{3,2,1,0:T(8,128)(2,1)S(1)} %all-gather.11), channel_id=2, replica_groups=mesh['row'=4,'col'=8] {'row'}, dimensions={0}, use_global_device_ids=true | all-gather | bytes 5242880 | tf_op jit(solution)/shard_map/all_gather | solution.py:534
  107.7 5.6 %all-to-all-start.1 = ((bf16[4,2,2,128,16,128]{5,4,3,2,1,0:T(8,128)(2,1)}), bf16[4,2,2,128,16,128]{5,4,3,2,1,0:T(8,128)(2,1)}, u32[]{:S(2)}, u32[]{:S(2)}) async-start(bf16[4,2,2,128,16,128]{5,4,3,2,1,0:T(8,128)(2,1)} %shard_map.60), calls=%async_computation.1 | async-start | bytes 16777216 | tf_op jit(solution)/shard_map/all_to_all | solution.py:518
  113.9 6.7 %bitcast_convert_fusion.g_ref = f32[128,128,128]{2,1,0:T(8,128)} fusion(f16[4,8,4,128,128]{4,3,2,1,0:T(8,128)(2,1)} %bitcast.116), kind=kLoop, calls=%fused_computation | loop fusion | flops 2097152 | bytes 12582912 | tf_op jit(solution)/shard_map/convert_element_type | solution.py:537
  120.6 6.2 %shard_map.62 = (f32[512,512]{1,0:T(8,128)}, f32[512,512]{1,0:T(8,128)}, f32[512,512]{1,0:T(8,128)}, f32[512,512]{1,0:T(8,128)}, f32[512,512]{1,0:T(8,128)}, /*index=5*/f32[512,512]{1,0:T(8,128)}) custom-call(f32[128,128,128]{2,1,0:T(8,128)} %bitcast_convert_fusion.g_ref), custom_call_target="tpu_custom_call" | custom-call | tf_op jit(solution)/shard_map/pallas_call | solution.py:200
  126.7 22.6 %shard_map.63 = (f32[512,512]{1,0:T(8,128)}, f32[512,512]{1,0:T(8,128)}, bf16[512,512]{1,0:T(8,128)(2,1)}) custom-call(f32[512,512]{1,0:T(8,128)} %get-tuple-element.49.d_ref), custom_call_target="tpu_custom_call" | custom-call | flops 30000001024 | bytes 4000000 | tf_op jit(solution)/shard_map/pallas_call | solution.py:234
  150.7 36.5 %collective-permute-done.2 = bf16[15,128,128]{2,1,0:T(8,128)(2,1)S(1)} collective-permute-done((bf16[15,128,128]{2,1,0:T(8,128)(2,1)S(1)}, bf16[15,128,128]{2,1,0:T(8,128)(2,1)S(1)}, u32[]{:S(2)}, u32[]{:S(2)}) %collective-permute-start.2) | collective-permute-done | bytes 491552 | tf_op jit(solution)/shard_map/ppermute | solution.py:475
  188.2 8.1 %shard_map.64 = (f32[512,512]{1,0:T(8,128)}, f32[512,512]{1,0:T(8,128)}, bf16[512,512]{1,0:T(8,128)(2,1)}, bf16[512,512]{1,0:T(8,128)(2,1)}, f32[512,512]{1,0:T(...) custom-call(f32[512,512]{1,0:T(8,128)} %get-tuple-element.50.v_ref.refs_6_, f32[512,512]{1,0:T(8,128)} %get-tuple-element.51.refs_0_, ...), custom_call_target="tpu_custom_call" | custom-call | flops 3000000000 | bytes 10000000 | tf_op jit(solution)/shard_map/pallas_call | solution.py:264
  196.3 22.8 %shard_map.65 = (f32[512,512]{1,0:T(8,128)}, f32[512,512]{1,0:T(8,128)}, bf16[512,512]{1,0:T(8,128)(2,1)}) custom-call(f32[512,512]{1,0:T(8,128)} %get-tuple-element.56.d_ref), custom_call_target="tpu_custom_call" | custom-call | flops 30000001024 | bytes 4000000 | tf_op jit(solution)/shard_map/pallas_call | solution.py:234
  219.1 4.8 %shard_map.66 = (f32[512,512]{1,0:T(8,128)}, bf16[512,512]{1,0:T(8,128)(2,1)}, f32[512,512]{1,0:T(8,128)}) custom-call(f32[512,512]{1,0:T(8,128)} %get-tuple-element.57.v_ref.refs_7_, f32[512,512]{1,0:T(8,128)} %get-tuple-element.58.refs_0_, f32[512,512]{1,0:T(8,128)} %get-tuple-element.59.refs_1_), custom_call_target="tpu_custom_call" | custom-call | flops 3000000000 | bytes 10000000 | tf_op jit(solution)/shard_map/pallas_call | solution.py:264
  223.9 4.9 %pad.8 = bf16[8,30,128,128]{3,2,1,0:T(8,128)(2,1)S(1)} pad(bf16[8,29,128,128]{3,2,1,0:T(8,128)(2,1)} %bitcast.118, bf16[]{:T(256)} %constant.142.clone.1), padding=0_0x1_0x0_0x0_0 | pad | bytes 15466498 | tf_op jit(solution)/shard_map/jit(_pad)/pad | solution.py:446
  232.8 22.7 %shard_map.67 = (f32[512,512]{1,0:T(8,128)}, f32[512,512]{1,0:T(8,128)}, bf16[512,512]{1,0:T(8,128)(2,1)}) custom-call(f32[512,512]{1,0:T(8,128)} %get-tuple-element.65.d_ref), custom_call_target="tpu_custom_call" | custom-call | flops 30000001024 | bytes 4000000 | tf_op jit(solution)/shard_map/pallas_call | solution.py:234
  265.7 9.8 %all-to-all-start.2 = ((bf16[8,4,2,128,128]{4,3,1,2,0:T(8,128)(2,1)}), bf16[8,4,2,128,128]{4,3,1,2,0:T(8,128)(2,1)}, u32[]{:S(2)}, u32[]{:S(2)}) async-start(bf16[8,4,2,128,128]{4,3,1,2,0:T(8,128)(2,1)} %copy.38), calls=%async_computation.2 | async-start | bytes 4194304 | tf_op jit(solution)/shard_map/all_to_all | solution.py:581
  275.5 3.6 collective-permute-done
  279.1 4.4 %broadcast_select_fusion = bf16[8,15,128,128]{3,2,1,0:T(8,128)(2,1)} fusion(bf16[8,15,128,128]{3,2,1,0:T(8,128)(2,1)} %collective-permute-done, bf16[8,15,128,128]{3,2,1,0:T(8,128)(2,1)} %fusion.1, pred[]{:T(512)S(6)} %eq.153), kind=kLoop, calls=%fused_computation.5 | loop fusion | flops 1966080 | bytes 11796481 | tf_op jit(solution)/shard_map/jit(_where)/select_n | solution.py:464
  286.7 13.4 %collective-permute-done.3 = bf16[4,15,128,128]{3,2,1,0:T(8,128)(2,1)} collective-permute-done((bf16[4,15,128,128]{3,2,1,0:T(8,128)(2,1)S(1)}, bf16[4,15,128,128]{3,2,1,0:T(8,128)(2,1)}, u32[]{:S(2)}, u32[]{:S(2)}) %collective-permute-start.3) | collective-permute-done | bytes 1966112 | tf_op jit(solution)/shard_map/ppermute | solution.py:463
  304.6 24.5 %shard_map.68.refs_9_ = bf16[4096,1536]{1,0:T(8,128)(2,1)} custom-call(bf16[8,29,128,128]{3,2,1,0:T(8,128)(2,1)} %bitcast.119, bf16[4,29,128,128]{3,2,1,0:T(8,128)(2,1)} %copy-done, bf16[512,512]{1,0:T(8,128)(2,1)} %get-tuple-element.70.refs_2_, bf16[512,512]{1,0:T(8,128)(2,1)} %get-tuple-element.71.refs_3_, bf16[512,512]{1,0:T(8,128)(2,1)} %get-tuple-element.72.refs_4_, ...), custom_call_target="tpu_custom_call" | custom-call | flops 17515413504 | bytes 25165824 | tf_op jit(solution)/shard_map/pallas_call | solution.py:358
  336.1 12.4 %shard_map.70 = f32[512,1536]{1,0:T(8,128)} custom-call(s32[2]{0:T(128)} %pad_add_fusion.2.ids_ref, f32[12,4,128,128]{3,2,1,0:T(8,128)} %pad_maximum_fusion.1.own_ref, f32[512,512]{1,0:T(8,128)} %get-tuple-element.79.refs_0_, f32[512,512]{1,0:T(8,128)} %get-tuple-element.80.refs_1_, f32[512,512]{1,0:T(8,128)} %get-tuple-element.81.refs_2_, ...), custom_call_target="tpu_custom_call" | custom-call | flops 6000000000 | bytes 15000000 | tf_op jit(solution)/shard_map/pallas_call | solution.py:307
  351.5 4.4 %broadcast_select_fusion.1.refs_0_ = bf16[8,15,128,128]{3,2,1,0:T(8,128)(2,1)} fusion(bf16[8,15,128,128]{3,2,1,0:T(8,128)(2,1)} %collective-permute-done.1, bf16[8,15,128,128]{3,2,1,0:T(8,128)(2,1)} %broadcast_select_fusion, pred[]{:T(512)S(6)} %eq.152), kind=kLoop, calls=%fused_computation.6 | loop fusion | flops 1966080 | bytes 11796481 | tf_op jit(solution)/shard_map/jit(_where)/select_n | solution.py:464
  355.9 62.5 %shard_map.69 = f32[65536,128]{1,0:T(8,128)} custom-call(s32[2]{0:T(128)} %pad_add_fusion.2.ids_ref, s32[2,32]{1,0:T(2,128)} %get-tuple-element.125.slot_ref, s32[2,32,128]{2,1,0:T(8,128)} %get-tuple-element.121.order_ref, bf16[8,15,128,128]{3,2,1,0:T(8,128)(2,1)} %broadcast_select_fusion.1.refs_0_, ...), custom_call_target="tpu_custom_call" | custom-call | flops 19327352832 | bytes 67108864 | tf_op jit(solution)/shard_map/pallas_call | solution.py:425
  (72 shorter events, 48.2 us)
Async XLA Ops:
  10.2 7.0 %copy-start.4 = (s32[2,16]{1,0:T(2,128)S(1)}, s32[2,16]{1,0:T(2,128)}, u32[]{:S(2)}) copy-start(s32[2,16]{1,0:T(2,128)} %map_ref.3) | copy-start | bytes 388
  13.6 18.8 %all-to-all-start = ((bf16[4,2,2,128,256]{4,3,2,1,0:T(8,128)(2,1)}), bf16[4,2,2,128,256]{4,3,2,1,0:T(8,128)(2,1)S(1)}, u32[]{:S(2)}, u32[]{:S(2)}) async-start(bf16[4,2,2,128,256]{4,3,2,1,0:T(8,128)(2,1)} %shard_map.59), calls=%async_computation | async-start | bytes 2097152 | tf_op jit(solution)/shard_map/all_to_all | solution.py:518
  17.1 206.7 %all-gather.8.cloned.1.call-start = ((), (), s32[]{:S(2)}) async-start(), calls=%async_computation.3 | async-start | bytes 8552448 | tf_op jit(solution)/shard_map/all_gather | solution.py:477
  17.2 8.1 %copy-start.5 = (s32[2,16,128]{2,1,0:T(8,128)S(1)}, s32[2,16,128]{2,1,0:T(8,128)}, u32[]{:S(2)}) copy-start(s32[2,16,128]{2,1,0:T(8,128)} %param.7) | copy-start | bytes 49156
  32.4 1.0 copy-start.1
  42.1 2.4 copy-start.3
  107.7 123.4 %all-to-all-start.1 = ((bf16[4,2,2,128,16,128]{5,4,3,2,1,0:T(8,128)(2,1)}), bf16[4,2,2,128,16,128]{5,4,3,2,1,0:T(8,128)(2,1)}, u32[]{:S(2)}, u32[]{:S(2)}) async-start(bf16[4,2,2,128,16,128]{5,4,3,2,1,0:T(8,128)(2,1)} %shard_map.60), calls=%async_computation.1 | async-start | bytes 16777216 | tf_op jit(solution)/shard_map/all_to_all | solution.py:518
  113.4 143.4 %all-gather.10.cloned.1.call-start = ((), (), s32[]{:S(2)}) async-start(), calls=%async_computation.4 | async-start | bytes 4423680 | tf_op jit(solution)/shard_map/all_gather | solution.py:477
  149.4 37.8 %collective-permute-start.2 = (bf16[15,128,128]{2,1,0:T(8,128)(2,1)S(1)}, bf16[15,128,128]{2,1,0:T(8,128)(2,1)S(1)}, u32[]{:S(2)}, u32[]{:S(2)}) collective-permute-start(bf16[15,128,128]{2,1,0:T(8,128)(2,1)S(1)} %slice_bitcast_fusion.7), channel_id=1, source_target_pairs={{0,4},{1,5},{2,6},{3,7},{8,12},{9,13},{10,14},{11,15},{16,20},{17,... | collective-permute-start | bytes 1474568 | tf_op jit(solution)/shard_map/ppermute | solution.py:475
  231.2 47.9 %collective-permute-start = (bf16[8,15,128,128]{3,2,1,0:T(8,128)(2,1)}, bf16[8,15,128,128]{3,2,1,0:T(8,128)(2,1)}, u32[]{:S(2)}, u32[]{:S(2)}) collective-permute-start(bf16[8,15,128,128]{3,2,1,0:T(8,128)(2,1)} %fusion.1), channel_id=1, source_target_pairs={{0,16},{4,20},{9,25},{13,29},{18,2},{22,6},{27,11},{31,15}} | collective-permute-start | bytes 11796488 | tf_op jit(solution)/shard_map/ppermute | solution.py:463
  260.6 1.8 copy-start
  262.5 1.6 copy-start.2
  262.7 37.4 %collective-permute-start.3 = (bf16[4,15,128,128]{3,2,1,0:T(8,128)(2,1)S(1)}, bf16[4,15,128,128]{3,2,1,0:T(8,128)(2,1)}, u32[]{:S(2)}, u32[]{:S(2)}) collective-permute-start(bf16[4,15,128,128]{3,2,1,0:T(8,128)(2,1)S(1)} %fusion.3), channel_id=1, source_target_pairs={{0,16},{4,20},{9,25},{13,29},{18,2},{22,6},{27,11},{31,15}} | collective-permute-start | bytes 5898248 | tf_op jit(solution)/shard_map/ppermute | solution.py:463
  265.7 65.8 %all-to-all-start.2 = ((bf16[8,4,2,128,128]{4,3,1,2,0:T(8,128)(2,1)}), bf16[8,4,2,128,128]{4,3,1,2,0:T(8,128)(2,1)}, u32[]{:S(2)}, u32[]{:S(2)}) async-start(bf16[8,4,2,128,128]{4,3,1,2,0:T(8,128)(2,1)} %copy.38), calls=%async_computation.2 | async-start | bytes 4194304 | tf_op jit(solution)/shard_map/all_to_all | solution.py:581
  283.5 68.0 %collective-permute-start.1 = (bf16[8,15,128,128]{3,2,1,0:T(8,128)(2,1)}, bf16[8,15,128,128]{3,2,1,0:T(8,128)(2,1)}, u32[]{:S(2)}, u32[]{:S(2)}) collective-permute-start(bf16[8,15,128,128]{3,2,1,0:T(8,128)(2,1)} %broadcast_select_fusion), channel_id=1, source_target_pairs={{0,8},{2,10},{4,12},{6,14},{9,1},{11,3},{13,5},{15,7},{16,24},{18,... | collective-permute-start | bytes 11796488 | tf_op jit(solution)/shard_map/ppermute | solution.py:463
  303.2 45.3 %collective-permute-start.4 = (bf16[4,15,128,128]{3,2,1,0:T(8,128)(2,1)}, bf16[4,15,128,128]{3,2,1,0:T(8,128)(2,1)S(1)}, u32[]{:S(2)}, u32[]{:S(2)}) collective-permute-start(bf16[4,15,128,128]{3,2,1,0:T(8,128)(2,1)} %broadcast_select_fusion.2), channel_id=1, source_target_pairs={{0,8},{2,10},{4,12},{6,14},{9,1},{11,3},{13,5},{15,7},{16,24},{18,... | collective-permute-start | bytes 5898248 | tf_op jit(solution)/shard_map/ppermute | solution.py:463
Sparse Core Ops, SparseCore 0:
  44.6 138.3 all-gather.7
  188.3 68.4 all-gather.9

commit v3 on v2

--- a/solution.py
+++ b/solution.py
@@ -346,33 +346,68 @@
 BELOW = STEPS * (STEPS - 1) // 2
 
 
-def solve_kernel(first, n_parts, *refs):
-    parts, blocks, out_ref = refs[:n_parts], refs[n_parts:-1], refs[-1]
-    solve_into(parts, blocks[:BELOW], blocks[BELOW:], out_ref, first)
-
-
-def solve_rows(parts, first, lower, inverse):
-    tile = parts[0].shape[-1]
-    count = parts[0].shape[1]
-    rows = (first + count) * tile
+def solve_kernel(begin, end, step, *refs):
+    row_refs, refs = refs[:step], refs[step:]
+    known, blocks, out_ref = refs[: min(begin, 1)], refs[min(begin, 1) : -1], refs[-1]
+    lower, inverse = blocks[:BELOW], blocks[BELOW:]
+    width = PWT * row_refs[0].shape[-1]
+    done = [known[0][:, q * width : (q + 1) * width] for q in range(begin)]
+    for s in range(begin, end):
+        columns = range((s - begin) * PWT, (s - begin + 1) * PWT)
+        rest = jnp.concatenate([side_by_side([ref[j] for j in columns]) for ref in row_refs], axis=0)
+        if s > 0:
+            rest = rest.astype(F32)
+            for q in range(s):
+                rest = rest - dot(done[q], lower[s * (s - 1) // 2 + q][...], NT)
+            rest = rest.astype(BF16)
+        done.append(dot(rest, inverse[s][...], NT).astype(BF16))
+        out_ref[:, (s - begin) * width : (s - begin + 1) * width] = done[s]
+
+
+def solve_rows(part, known, begin, lower, inverse):
+    tile = part.shape[-1]
+    step = 4
+    steps = -(-part.shape[1] // step)
+    end = begin + part.shape[0] // PWT
+    width = PWT * tile
+    rows = step * tile
+    known = [known] if begin else []
+    held = (*lower, *inverse)
+
+    def row_tile(k):
+        last = part.shape[1] - 1
+        return pl.BlockSpec(
+            (part.shape[0], 1, tile, tile), lambda i: (0, jnp.minimum(i * step + k, last), 0, 0)
+        )
+
     return pl.pallas_call(
-        functools.partial(solve_kernel, first, len(parts)),
-        out_shape=jax.ShapeDtypeStruct((rows, TILES * tile), BF16),
+        functools.partial(solve_kernel, begin, end, step),
+        out_shape=jax.ShapeDtypeStruct((steps * rows, (end - begin) * width), BF16),
+        grid=(steps,),
+        in_specs=[row_tile(k) for k in range(step)]
+        + [pl.BlockSpec((rows, k.shape[1]), lambda i: (i, 0)) for k in known]
+        + [whole(x.shape) for x in held],
+        out_specs=pl.BlockSpec((rows, (end - begin) * width), lambda i: (i, 0)),
         compiler_params=pltpu.CompilerParams(vmem_limit_bytes=VMEM_LIMIT),
         cost_estimate=pl.CostEstimate(
-            flops=count * tile * (TILES * tile) ** 2 * 2,
-            bytes_accessed=4 * rows * TILES * tile,
+            flops=2 * steps * rows * (end - begin) * width * end * width,
+            bytes_accessed=4 * part.size,
             transcendentals=0,
         ),
-    )(*parts, *lower, *inverse)
+    )(*[part] * step, *known, *held)
 
 
 def final_kernel(row_count, col_count, n_parts, ids_ref, slot_ref, order_ref, *refs):
     parts, blocks = refs[:n_parts], refs[n_parts : n_parts + BELOW + STEPS]
-    recv_ref, xr_ref, front_ref, out_ref, xc_ref = refs[n_parts + BELOW + STEPS :]
+    rest = refs[n_parts + BELOW + STEPS :]
+    recv_ref, row_refs, (front_ref, out_ref, xc_ref, xr_ref) = rest[0], rest[1:-4], rest[-4:]
     g = pl.program_id(0)
     tile = out_ref.shape[-1]
     share = xr_ref.shape[0] // tile
+    for n, ref in enumerate(row_refs):
+        k = n % share
+        left = 0 if n < share else row_refs[0].shape[1]
+        xr_ref[k * tile : (k + 1) * tile, left : left + ref.shape[1]] = ref[...]
     local_cols = xc_ref.shape[0] // tile
 
     @pl.when(g == 0)
@@ -418,10 +453,21 @@
                 )
 
 
-def final_update(ids, slots, order, parts, lower, inverse, received, xr, front, row_count, col_count):
+def final_update(
+    ids, slots, order, parts, lower, inverse, received, solved, first, front, row_count, col_count
+):
     rows = front.shape[0] // col_count
-    block = pl.BlockSpec((rows, front.shape[1]), lambda g, *_: (g, 0))
+    tile = front.shape[1]
+    share = slots.shape[1] // col_count
+    wide = sum(x.shape[1] for x in solved)
+    block = pl.BlockSpec((rows, tile), lambda g, *_: (g, 0))
     held = (*parts, *lower, *inverse, received)
+
+    def row_tile(k, x):
+        return pl.BlockSpec(
+            (tile, x.shape[1]), lambda g, *_: (jnp.maximum(g * share + k - first, 0), 0)
+        )
+
     return pl.pallas_call(
         functools.partial(final_kernel, row_count, col_count, len(parts)),
         out_shape=jax.ShapeDtypeStruct(front.shape, F32),
@@ -429,15 +475,19 @@
             num_scalar_prefetch=3,
             grid=(col_count,),
             in_specs=[whole(x.shape) for x in held]
-            + [pl.BlockSpec((xr.shape[0] // col_count, xr.shape[1]), lambda g, *_: (g, 0)), block],
+            + [row_tile(k, x) for x in solved for k in range(share)]
+            + [block],
             out_specs=block,
-            scratch_shapes=[pltpu.VMEM((received.shape[2] * front.shape[1], xr.shape[1]), BF16)],
+            scratch_shapes=[
+                pltpu.VMEM((received.shape[2] * tile, wide), BF16),
+                pltpu.VMEM((share * tile, wide), BF16),
+            ],
         ),
         compiler_params=pltpu.CompilerParams(vmem_limit_bytes=VMEM_LIMIT),
         cost_estimate=pl.CostEstimate(
-            flops=2 * xr.size * xr.shape[1], bytes_accessed=8 * front.size, transcendentals=0
+            flops=2 * slots.shape[1] * tile * wide * wide, bytes_accessed=8 * front.size, transcendentals=0
         ),
-    )(ids, slots, order, *held, xr, front)
+    )(ids, slots, order, *held, *[x for x in solved for _ in range(share)], front)
 
 
 def column_rows(part, first, local_cols, row_count, col_count, col_dev):
@@ -534,7 +584,10 @@
     lead = lax.all_gather(lead, "row")
     lead, far = lax.optimization_barrier((lead, far))
     far = exchange(far)
-    blocks = unpack_lead(lead.reshape(-1, tile, tile).astype(F32), row_count, col_count, places)
+    blocks = list(unpack_lead(lead.reshape(-1, tile, tile).astype(F32), row_count, col_count, places))
+    if lead_cols > 1:
+        later, blocks[0] = lax.optimization_barrier((high, blocks[0]))
+        late = gather_columns(later, lead_cols - 1, first, col_count, col_dev)
 
     diagonals, inverses, inverses_b, lower, lower_b = [], [], [], {}, {}
     sent = []
@@ -547,9 +600,6 @@
         diagonals.append(c)
         inverses.append(v)
         inverses_b.append(vb)
-        if s == 0 and lead_cols > 1:
-            later, _ = lax.optimization_barrier((high, vb))
-            late = gather_columns(later, lead_cols - 1, first, col_count, col_dev)
         left = STEPS - 1 - s
         if left:
             index = lambda t, u: t * (t + 1) // 2 + u
@@ -565,15 +615,29 @@
     ]
     below_b = [lower_b[t, u] for t in range(1, STEPS) for u in range(t)]
 
+    solved = [solve_rows(parts[0], None, 0, below_b, inverses_b)]
     if lead_cols > 1:
-        late, inverses_b[-1] = lax.optimization_barrier((late, inverses_b[-1]))
+        late, inverses_b[-1], solved[0] = lax.optimization_barrier((late, inverses_b[-1], solved[0]))
         parts.append(merge_columns(late, lead_cols - 1, height, col_count))
         picked = column_rows(parts[-1], first, local_cols, row_count, col_count, col_dev)
         inverses_b[-1], picked = lax.optimization_barrier((inverses_b[-1], picked))
         sent.append(from_owner_row(picked, row_count, col_count, row_dev, col_dev))
-    xr = solve_rows(parts, first, below_b, inverses_b)
+        solved.append(
+            solve_rows(parts[1], solved[0], parts[0].shape[0] // PWT, below_b, inverses_b)
+        )
     schur_part = final_update(
-        ids, slots, jnp.maximum(orders, 0), sent, below_b, inverses_b, far, xr, front, row_count, col_count
+        ids,
+        slots,
+        jnp.maximum(orders, 0),
+        sent,
+        below_b,
+        inverses_b,
+        far,
+        solved,
+        first,
+        front,
+        row_count,
+        col_count,
     )
 
     low, parts = lax.optimization_barrier((low, parts))

time: 431 us -> 422 us (0.979)
  waiting for transfers between devices: 54.9 us -> 39.3 us
    ppermute x1, waiting for transfers between devices: 36.5 us -> 20.3 us  [gather_columns(): lax.ppermute(rows[n - half:], 'col', [(c, c + count) for c in range(count)])]
    pallas_call x1 -> x2, Pallas kernels: 24.5 us -> 26.8 us  [solve_rows(): pl.pallas_call(functools.partial(solve_kernel, begin, end, step), out_sha...]
  transfers between devices with their start and end apart: 10 -> 10, of which waited for: 4 -> 3; matrix products, arithmetic and copies ran while one was open for 11% -> 13% of each run, Pallas kernels for 31% -> 32%
where the time goes in v3:
time: 422 us; the launch traced here: 415 us
  Pallas kernels  210 us (50%)
  blocking collectives  62.2 us (15%)
  waiting for transfers between devices  39.3 us (9%)
  other arithmetic  36.5 us (9%)
  local copies, waits for them, and re-layouts  27.5 us (7%)
  starting transfers between devices  24.5 us (6%)
  between operations  14.8 us (4%)
    pallas_call x3, Pallas kernels, factor_block(): pl.pallas_call(block_kernel, out_shape=(jax.ShapeDtypeStruct(shape, F32),...  68.3 us
    pallas_call x1, Pallas kernels, final_update(): pl.pallas_call(functools.partial(final_kernel, row_count, col_count, len(...  64.1 us
    all_gather x1, blocking collectives, shards(): lead = lax.all_gather(lead, 'col')  34.5 us
    all_gather x1, blocking collectives, shards(): lead = lax.all_gather(lead, 'row')  27.8 us
    pallas_call x2, Pallas kernels, solve_rows(): pl.pallas_call(functools.partial(solve_kernel, begin, end, step), out_sha...  26.8 us
    ppermute x1, waiting for transfers between devices, gather_columns(): lax.ppermute(rows[n - half:], 'col', [(c, c + count) for c in range(count)])  20.3 us
    ppermute x4, waiting for transfers between devices, from_owner_row(): arrived = lax.ppermute(own, ('row', 'col'), pairs)  16.3 us
    select_n x4, other arithmetic, from_owner_row(): own = jnp.where(away % (2 * stride) == stride, arrived, own)  14.9 us
  transfers between devices with their start and end apart: 10, of which 3 were waited for; matrix products, arithmetic and copies ran while one was open for 13% of the time, Pallas kernels for 32%

profile of v3, /device:TPU:24, one launch (start us, length us, event | category | flops | bytes accessed | tf_op | source)
XLA Modules:
  0.0 414.7 jit_solution(14954579193853125230)
XLA Ops:
  13.6 3.5 all-to-all-start
  17.2 7.6 %shard_map.60 = bf16[4,2,2,128,16,128]{5,4,3,2,1,0:T(8,128)(2,1)} custom-call(s32[2]{0:T(128)} %pad_add_fusion.2.ids_ref, s32[2,16]{1,0:T(2,128)} %map_ref.3, bf16[2,4,128,16,128]{4,3,2,1,0:T(8,128)(2,1)} %bitcast.127), custom_call_target="tpu_custom_call" | custom-call | tf_op jit(solution)/shard_map/pallas_call | solution.py:123
  27.6 4.7 %fusion.19 = (f32[32,1,128,1,1,128]{5,4,3,2,1,0:T(1,128)}, f32[32,1,128,1,1,128]{5,4,3,2,1,0:T(1,128)}) fusion(f32[32,1,128,16,1,128]{5,4,3,2,1,0:T(1,128)} %param.4), kind=kLoop, calls=%fused_computation.95 | loop fusion | bytes 8388608 | tf_op jit(solution)/shard_map/slice | solution.py:576
  33.3 8.6 %shard_map.61 = (bf16[32,2,128,128]{3,2,1,0:T(8,128)(2,1)}, bf16[32,2,128,128]{3,2,1,0:T(8,128)(2,1)}) custom-call(s32[2,32]{1,0:T(2,128)} %get-tuple-element.128.slot_ref, f32[32,128,128]{2,1,0:T(8,128)} %bitcast.125, f32[32,128,128]{2,1,0:T(8,128)} %bitcast.124, s32[32,2,128]{2,1,0:T(2,128)} %copy.32.refs_2_, bf16[16,128,256]{2,1,0:T(8,128)(2,1)} %bitcast.128), custom_call_target="tpu_custom_call" | custom-call | tf_op jit(solution)/shard_map/pallas_call | solution.py:158
  45.2 34.5 %all-gather.11 = f16[8,4,128,128]{3,2,1,0:T(8,128)(2,1)S(1)} all-gather(f16[1,4,128,128]{3,2,1,0:T(8,128)(2,1)S(1)} %pad_maximum_fusion.2), channel_id=1, replica_groups=mesh['row'=4,'col'=8] {'col'}, dimensions={0}, use_global_device_ids=true | all-gather | bytes 1179648 | tf_op jit(solution)/shard_map/all_gather | solution.py:581
  79.7 27.8 %all-gather.12 = f16[32,4,128,128]{3,2,1,0:T(8,128)(2,1)} all-gather(f16[8,4,128,128]{3,2,1,0:T(8,128)(2,1)S(1)} %all-gather.11), channel_id=2, replica_groups=mesh['row'=4,'col'=8] {'row'}, dimensions={0}, use_global_device_ids=true | all-gather | bytes 5242880 | tf_op jit(solution)/shard_map/all_gather | solution.py:584
  107.5 5.6 %all-to-all-start.1 = ((bf16[4,2,2,128,16,128]{5,4,3,2,1,0:T(8,128)(2,1)}), bf16[4,2,2,128,16,128]{5,4,3,2,1,0:T(8,128)(2,1)}, u32[]{:S(2)}, u32[]{:S(2)}) async-start(bf16[4,2,2,128,16,128]{5,4,3,2,1,0:T(8,128)(2,1)} %shard_map.60), calls=%async_computation.1 | async-start | bytes 16777216 | tf_op jit(solution)/shard_map/all_to_all | solution.py:568
  113.2 6.6 %bitcast_convert_fusion.g_ref = f32[128,128,128]{2,1,0:T(8,128)} fusion(f16[4,8,4,128,128]{4,3,2,1,0:T(8,128)(2,1)} %bitcast.122), kind=kLoop, calls=%fused_computation | loop fusion | flops 2097152 | bytes 12582912 | tf_op jit(solution)/shard_map/convert_element_type | solution.py:587
  119.8 6.2 %shard_map.62 = (f32[512,512]{1,0:T(8,128)}, f32[512,512]{1,0:T(8,128)}, f32[512,512]{1,0:T(8,128)}, f32[512,512]{1,0:T(8,128)}, f32[512,512]{1,0:T(8,128)}, /*index=5*/f32[512,512]{1,0:T(8,128)}) custom-call(f32[128,128,128]{2,1,0:T(8,128)} %bitcast_convert_fusion.g_ref), custom_call_target="tpu_custom_call" | custom-call | tf_op jit(solution)/shard_map/pallas_call | solution.py:200
  128.5 22.7 %shard_map.63 = (f32[512,512]{1,0:T(8,128)}, f32[512,512]{1,0:T(8,128)}, bf16[512,512]{1,0:T(8,128)(2,1)}) custom-call(f32[512,512]{1,0:T(8,128)} %get-tuple-element.52.d_ref), custom_call_target="tpu_custom_call" | custom-call | flops 30000001024 | bytes 4000000 | tf_op jit(solution)/shard_map/pallas_call | solution.py:234
  151.2 8.1 %shard_map.64 = (f32[512,512]{1,0:T(8,128)}, f32[512,512]{1,0:T(8,128)}, bf16[512,512]{1,0:T(8,128)(2,1)}, bf16[512,512]{1,0:T(8,128)(2,1)}, f32[512,512]{1,0:T(...) custom-call(f32[512,512]{1,0:T(8,128)} %get-tuple-element.53.v_ref.refs_6_, f32[512,512]{1,0:T(8,128)} %get-tuple-element.54.refs_0_, ...), custom_call_target="tpu_custom_call" | custom-call | flops 3000000000 | bytes 10000000 | tf_op jit(solution)/shard_map/pallas_call | solution.py:264
  159.4 20.3 %collective-permute-done.2 = bf16[15,128,128]{2,1,0:T(8,128)(2,1)S(1)} collective-permute-done((bf16[15,128,128]{2,1,0:T(8,128)(2,1)S(1)}, bf16[15,128,128]{2,1,0:T(8,128)(2,1)S(1)}, u32[]{:S(2)}, u32[]{:S(2)}) %collective-permute-start.2) | collective-permute-done | bytes 491552 | tf_op jit(solution)/shard_map/ppermute | solution.py:525
  181.7 22.9 %shard_map.65 = (f32[512,512]{1,0:T(8,128)}, f32[512,512]{1,0:T(8,128)}, bf16[512,512]{1,0:T(8,128)(2,1)}) custom-call(f32[512,512]{1,0:T(8,128)} %get-tuple-element.59.d_ref), custom_call_target="tpu_custom_call" | custom-call | flops 30000001024 | bytes 4000000 | tf_op jit(solution)/shard_map/pallas_call | solution.py:234
  204.6 4.8 %shard_map.66 = (f32[512,512]{1,0:T(8,128)}, bf16[512,512]{1,0:T(8,128)(2,1)}, f32[512,512]{1,0:T(8,128)}) custom-call(f32[512,512]{1,0:T(8,128)} %get-tuple-element.60.v_ref.refs_7_, f32[512,512]{1,0:T(8,128)} %get-tuple-element.61.refs_0_, f32[512,512]{1,0:T(8,128)} %get-tuple-element.62.refs_1_), custom_call_target="tpu_custom_call" | custom-call | flops 3000000000 | bytes 10000000 | tf_op jit(solution)/shard_map/pallas_call | solution.py:264
  209.4 4.9 %pad.8 = bf16[8,30,128,128]{3,2,1,0:T(8,128)(2,1)S(1)} pad(bf16[8,29,128,128]{3,2,1,0:T(8,128)(2,1)} %bitcast.113, bf16[]{:T(256)} %constant.142.clone.1), padding=0_0x1_0x0_0x0_0 | pad | bytes 15466498 | tf_op jit(solution)/shard_map/jit(_pad)/pad | solution.py:496
  218.1 22.7 %shard_map.67 = (f32[512,512]{1,0:T(8,128)}, f32[512,512]{1,0:T(8,128)}, bf16[512,512]{1,0:T(8,128)(2,1)}) custom-call(f32[512,512]{1,0:T(8,128)} %get-tuple-element.67.d_ref), custom_call_target="tpu_custom_call" | custom-call | flops 30000001024 | bytes 4000000 | tf_op jit(solution)/shard_map/pallas_call | solution.py:234
  240.8 13.3 %shard_map.68.refs_4_.refs_9_.refs_10_.refs_11_.refs_12_ = bf16[4096,1024]{1,0:T(8,128)(2,1)} custom-call(bf16[8,29,128,128]{3,2,1,0:T(8,128)(2,1)} %bitcast.114, bf16[8,29,128,128]{3,2,1,0:T(8,128)(2,1)} %bitcast.115, bf16[8,29,128,128]{3,2,1,0:T(8,128)(2,1)} %bitcast.116, bf16[8,29,128,128]{3,2,1,0:T(8,128)(2,1)} %bitcast.117, ...), custom_call_target="tpu_custom_call" | custom-call | flops 8589934592 | bytes 15204352 | tf_op jit(solution)/shard_map/pallas_call | solution.py:383
  264.1 6.4 %all-to-all-start.2 = ((bf16[8,4,2,128,128]{4,3,1,2,0:T(8,128)(2,1)}), bf16[8,4,2,128,128]{4,3,1,2,0:T(8,128)(2,1)}, u32[]{:S(2)}, u32[]{:S(2)}) async-start(bf16[8,4,2,128,128]{4,3,1,2,0:T(8,128)(2,1)} %copy.38), calls=%async_computation.2 | async-start | bytes 4194304 | tf_op jit(solution)/shard_map/all_to_all | solution.py:645
  274.4 4.5 %broadcast_select_fusion = bf16[8,15,128,128]{3,2,1,0:T(8,128)(2,1)} fusion(bf16[8,15,128,128]{3,2,1,0:T(8,128)(2,1)} %collective-permute-done, bf16[8,15,128,128]{3,2,1,0:T(8,128)(2,1)} %fusion.1, pred[]{:T(512)S(6)} %eq.153), kind=kLoop, calls=%fused_computation.5 | loop fusion | flops 1966080 | bytes 11796481 | tf_op jit(solution)/shard_map/jit(_where)/select_n | solution.py:514
  283.4 16.3 %collective-permute-done.3 = bf16[4,15,128,128]{3,2,1,0:T(8,128)(2,1)} collective-permute-done((bf16[4,15,128,128]{3,2,1,0:T(8,128)(2,1)S(1)}, bf16[4,15,128,128]{3,2,1,0:T(8,128)(2,1)}, u32[]{:S(2)}, u32[]{:S(2)}) %collective-permute-start.3) | collective-permute-done | bytes 1966112 | tf_op jit(solution)/shard_map/ppermute | solution.py:513
  305.3 13.5 %shard_map.69.refs_13_.refs_14_.refs_15_.refs_16_ = bf16[4096,512]{1,0:T(8,128)(2,1)} custom-call(bf16[4,29,128,128]{3,2,1,0:T(8,128)(2,1)} %pad_maximum_fusion.refs_0_.refs_1_.refs_2_.refs_3_, bf16[4,29,128,128]{3,2,1,0:T(8,128)(2,1)} %pad_maximum_fusion.refs_0_.refs_1_.refs_2_.refs_3_, ...), custom_call_target="tpu_custom_call" | custom-call | flops 6442450944 | bytes 7602176 | tf_op jit(solution)/shard_map/pallas_call | solution.py:383
  323.4 12.4 %shard_map.71 = f32[512,1536]{1,0:T(8,128)} custom-call(s32[2]{0:T(128)} %pad_add_fusion.2.ids_ref, f32[12,4,128,128]{3,2,1,0:T(8,128)} %pad_maximum_fusion.1.own_ref, f32[512,512]{1,0:T(8,128)} %get-tuple-element.83.refs_0_, f32[512,512]{1,0:T(8,128)} %get-tuple-element.84.refs_1_, f32[512,512]{1,0:T(8,128)} %get-tuple-element.85.refs_2_, ...), custom_call_target="tpu_custom_call" | custom-call | flops 6000000000 | bytes 15000000 | tf_op jit(solution)/shard_map/pallas_call | solution.py:307
  338.8 4.5 %broadcast_select_fusion.1.refs_0_ = bf16[8,15,128,128]{3,2,1,0:T(8,128)(2,1)} fusion(bf16[8,15,128,128]{3,2,1,0:T(8,128)(2,1)} %collective-permute-done.1, bf16[8,15,128,128]{3,2,1,0:T(8,128)(2,1)} %broadcast_select_fusion, pred[]{:T(512)S(6)} %eq.152), kind=kLoop, calls=%fused_computation.6 | loop fusion | flops 1966080 | bytes 11796481 | tf_op jit(solution)/shard_map/jit(_where)/select_n | solution.py:514
  343.3 64.1 %shard_map.70 = f32[65536,128]{1,0:T(8,128)} custom-call(s32[2]{0:T(128)} %pad_add_fusion.2.ids_ref, s32[2,32]{1,0:T(2,128)} %get-tuple-element.129.slot_ref, s32[2,32,128]{2,1,0:T(8,128)} %get-tuple-element.125.order_ref, bf16[8,15,128,128]{3,2,1,0:T(8,128)(2,1)} %broadcast_select_fusion.1.refs_0_, ...), custom_call_target="tpu_custom_call" | custom-call | flops 19327352832 | bytes 67108864 | tf_op jit(solution)/shard_map/pallas_call | solution.py:471
  (69 shorter events, 53.2 us)
Async XLA Ops:
  7.2 10.0 %copy-start.2 = (s32[2,16]{1,0:T(2,128)S(1)}, s32[2,16]{1,0:T(2,128)}, u32[]{:S(2)}) copy-start(s32[2,16]{1,0:T(2,128)} %map_ref.3) | copy-start | bytes 388
  13.6 18.7 %all-to-all-start = ((bf16[4,2,2,128,256]{4,3,2,1,0:T(8,128)(2,1)}), bf16[4,2,2,128,256]{4,3,2,1,0:T(8,128)(2,1)S(1)}, u32[]{:S(2)}, u32[]{:S(2)}) async-start(bf16[4,2,2,128,256]{4,3,2,1,0:T(8,128)(2,1)} %shard_map.59), calls=%async_computation | async-start | bytes 2097152 | tf_op jit(solution)/shard_map/all_to_all | solution.py:568
  17.1 192.3 %all-gather.8.cloned.1.call-start = ((), (), s32[]{:S(2)}) async-start(), calls=%async_computation.3 | async-start | bytes 8552448 | tf_op jit(solution)/shard_map/all_gather | solution.py:527
  17.2 8.1 %copy-start.3 = (s32[2,16,128]{2,1,0:T(8,128)S(1)}, s32[2,16,128]{2,1,0:T(8,128)}, u32[]{:S(2)}) copy-start(s32[2,16,128]{2,1,0:T(8,128)} %param.7) | copy-start | bytes 49156
  32.3 1.0 copy-start
  107.5 109.2 %all-to-all-start.1 = ((bf16[4,2,2,128,16,128]{5,4,3,2,1,0:T(8,128)(2,1)}), bf16[4,2,2,128,16,128]{5,4,3,2,1,0:T(8,128)(2,1)}, u32[]{:S(2)}, u32[]{:S(2)}) async-start(bf16[4,2,2,128,16,128]{5,4,3,2,1,0:T(8,128)(2,1)} %shard_map.60), calls=%async_computation.1 | async-start | bytes 16777216 | tf_op jit(solution)/shard_map/all_to_all | solution.py:568
  113.1 143.6 %all-gather.10.cloned.1.call-start = ((), (), s32[]{:S(2)}) async-start(), calls=%async_computation.4 | async-start | bytes 4423680 | tf_op jit(solution)/shard_map/all_gather | solution.py:527
  127.0 52.7 %collective-permute-start.2 = (bf16[15,128,128]{2,1,0:T(8,128)(2,1)S(1)}, bf16[15,128,128]{2,1,0:T(8,128)(2,1)S(1)}, u32[]{:S(2)}, u32[]{:S(2)}) collective-permute-start(bf16[15,128,128]{2,1,0:T(8,128)(2,1)S(1)} %slice_bitcast_fusion.7), channel_id=1, source_target_pairs={{0,4},{1,5},{2,6},{3,7},{8,12},{9,13},{10,14},{11,15},{16,20},{17,... | collective-permute-start | bytes 1474568 | tf_op jit(solution)/shard_map/ppermute | solution.py:525
  216.7 57.7 %collective-permute-start = (bf16[8,15,128,128]{3,2,1,0:T(8,128)(2,1)}, bf16[8,15,128,128]{3,2,1,0:T(8,128)(2,1)}, u32[]{:S(2)}, u32[]{:S(2)}) collective-permute-start(bf16[8,15,128,128]{3,2,1,0:T(8,128)(2,1)} %fusion.1), channel_id=1, source_target_pairs={{0,16},{4,20},{9,25},{13,29},{18,2},{22,6},{27,11},{31,15}} | collective-permute-start | bytes 11796488 | tf_op jit(solution)/shard_map/ppermute | solution.py:513
  260.2 2.3 copy-start.1
  264.1 54.7 %all-to-all-start.2 = ((bf16[8,4,2,128,128]{4,3,1,2,0:T(8,128)(2,1)}), bf16[8,4,2,128,128]{4,3,1,2,0:T(8,128)(2,1)}, u32[]{:S(2)}, u32[]{:S(2)}) async-start(bf16[8,4,2,128,128]{4,3,1,2,0:T(8,128)(2,1)} %copy.38), calls=%async_computation.2 | async-start | bytes 4194304 | tf_op jit(solution)/shard_map/all_to_all | solution.py:645
  273.1 26.6 %collective-permute-start.3 = (bf16[4,15,128,128]{3,2,1,0:T(8,128)(2,1)S(1)}, bf16[4,15,128,128]{3,2,1,0:T(8,128)(2,1)}, u32[]{:S(2)}, u32[]{:S(2)}) collective-permute-start(bf16[4,15,128,128]{3,2,1,0:T(8,128)(2,1)S(1)} %fusion.3), channel_id=1, source_target_pairs={{0,16},{4,20},{9,25},{13,29},{18,2},{22,6},{27,11},{31,15}} | collective-permute-start | bytes 5898248 | tf_op jit(solution)/shard_map/ppermute | solution.py:513
  278.9 60.0 %collective-permute-start.1 = (bf16[8,15,128,128]{3,2,1,0:T(8,128)(2,1)}, bf16[8,15,128,128]{3,2,1,0:T(8,128)(2,1)}, u32[]{:S(2)}, u32[]{:S(2)}) collective-permute-start(bf16[8,15,128,128]{3,2,1,0:T(8,128)(2,1)} %broadcast_select_fusion), channel_id=1, source_target_pairs={{0,8},{2,10},{4,12},{6,14},{9,1},{11,3},{13,5},{15,7},{16,24},{18,... | collective-permute-start | bytes 11796488 | tf_op jit(solution)/shard_map/ppermute | solution.py:513
  302.7 33.1 %collective-permute-start.4 = (bf16[4,15,128,128]{3,2,1,0:T(8,128)(2,1)}, bf16[4,15,128,128]{3,2,1,0:T(8,128)(2,1)S(1)}, u32[]{:S(2)}, u32[]{:S(2)}) collective-permute-start(bf16[4,15,128,128]{3,2,1,0:T(8,128)(2,1)} %broadcast_select_fusion.2), channel_id=1, source_target_pairs={{0,8},{2,10},{4,12},{6,14},{9,1},{11,3},{13,5},{15,7},{16,24},{18,... | collective-permute-start | bytes 5898248 | tf_op jit(solution)/shard_map/ppermute | solution.py:513
Sparse Core Ops, SparseCore 0:
  44.4 140.4 all-gather.7
  187.1 69.5 all-gather.9

commit v4 on v3

--- a/solution.py
+++ b/solution.py
@@ -400,10 +400,11 @@
 def final_kernel(row_count, col_count, n_parts, ids_ref, slot_ref, order_ref, *refs):
     parts, blocks = refs[:n_parts], refs[n_parts : n_parts + BELOW + STEPS]
     rest = refs[n_parts + BELOW + STEPS :]
-    recv_ref, row_refs, (front_ref, out_ref, xc_ref, xr_ref) = rest[0], rest[1:-4], rest[-4:]
+    front_ref, out_ref, xc_ref, xr_ref = rest[-4:]
     g = pl.program_id(0)
     tile = out_ref.shape[-1]
     share = xr_ref.shape[0] // tile
+    kid_refs, row_refs = rest[: 2 * share], rest[2 * share : -4]
     for n, ref in enumerate(row_refs):
         k = n % share
         left = 0 if n < share else row_refs[0].shape[1]
@@ -421,12 +422,12 @@
             slot = slot_ref[h, a]
 
             @pl.when(slot >= 0)
-            def _(a=a, k=k, h=h, slot=slot):
+            def _(a=a, k=k, h=h):
                 @pl.loop(0, tile, unroll=8)
                 def _(t):
                     at = (k * tile + order_ref[h, a, t]) * local_cols
                     at = pl.ds(pl.multiple_of(at, local_cols), local_cols)
-                    out_ref[at, :] += recv_ref[slot, t].astype(F32)
+                    out_ref[at, :] += kid_refs[2 * k + h][0, t].astype(F32)
 
     last = row_count * (g * share + share - 1) + ids_ref[0]
     pair = 2 if local_cols % 2 == 0 else 1
@@ -461,7 +462,13 @@
     share = slots.shape[1] // col_count
     wide = sum(x.shape[1] for x in solved)
     block = pl.BlockSpec((rows, tile), lambda g, *_: (g, 0))
-    held = (*parts, *lower, *inverse, received)
+    held = (*parts, *lower, *inverse)
+
+    def kid_tile(k, h):
+        return pl.BlockSpec(
+            (1,) + received.shape[1:],
+            lambda g, ids, slots, order: (jnp.maximum(slots[h, g * share + k], 0), 0, 0, 0),
+        )
 
     def row_tile(k, x):
         return pl.BlockSpec(
@@ -475,6 +482,7 @@
             num_scalar_prefetch=3,
             grid=(col_count,),
             in_specs=[whole(x.shape) for x in held]
+            + [kid_tile(k, h) for k in range(share) for h in range(2)]
             + [row_tile(k, x) for x in solved for k in range(share)]
             + [block],
             out_specs=block,
@@ -487,7 +495,15 @@
         cost_estimate=pl.CostEstimate(
             flops=2 * slots.shape[1] * tile * wide * wide, bytes_accessed=8 * front.size, transcendentals=0
         ),
-    )(ids, slots, order, *held, *[x for x in solved for _ in range(share)], front)
+    )(
+        ids,
+        slots,
+        order,
+        *held,
+        *[received] * (2 * share),
+        *[x for x in solved for _ in range(share)],
+        front,
+    )
 
 
 def column_rows(part, first, local_cols, row_count, col_count, col_dev):
@@ -501,7 +517,7 @@
     return picked
 
 
-def from_owner_row(own, row_count, col_count, row_dev, col_dev):
+def from_owner_row(own, row_count, col_count, row_dev, col_dev, gate=None):
     away = row_dev ^ (col_dev % row_count)
     stride = row_count // 2
     while stride:
@@ -511,6 +527,8 @@
                 if (r ^ (c % row_count)) % (2 * stride) == 0:
                     pairs.append((r * col_count + c, (r ^ stride) * col_count + c))
         arrived = lax.ppermute(own, ("row", "col"), pairs)
+        if gate is not None:
+            arrived, gate = lax.optimization_barrier((arrived, gate))
         own = jnp.where(away % (2 * stride) == stride, arrived, own)
         stride //= 2
     return own
@@ -621,10 +639,10 @@
         parts.append(merge_columns(late, lead_cols - 1, height, col_count))
         picked = column_rows(parts[-1], first, local_cols, row_count, col_count, col_dev)
         inverses_b[-1], picked = lax.optimization_barrier((inverses_b[-1], picked))
-        sent.append(from_owner_row(picked, row_count, col_count, row_dev, col_dev))
         solved.append(
             solve_rows(parts[1], solved[0], parts[0].shape[0] // PWT, below_b, inverses_b)
         )
+        sent.append(from_owner_row(picked, row_count, col_count, row_dev, col_dev, solved[1]))
     schur_part = final_update(
         ids,
         slots,

time: 422 us -> 422 us (level)
  the two profiles are of different devices: /device:TPU:24 before, /device:TPU:6 now
where the time goes in v4:
time: 422 us; the launch traced here: 414 us
  Pallas kernels  209 us (50%)
  blocking collectives  62.5 us (15%)
  waiting for transfers between devices  37.6 us (9%)
  other arithmetic  35.1 us (8%)
  local copies, waits for them, and re-layouts  27.7 us (7%)
  starting transfers between devices  27.5 us (7%)
  between operations  14.8 us (4%)
    pallas_call x3, Pallas kernels, factor_block(): pl.pallas_call(block_kernel, out_shape=(jax.ShapeDtypeStruct(shape, F32),...  68.4 us
    pallas_call x1, Pallas kernels, final_update(): pl.pallas_call(functools.partial(final_kernel, row_count, col_count, len(...  63.4 us
    all_gather x1, blocking collectives, shards(): lead = lax.all_gather(lead, 'col')  36.3 us
    pallas_call x2, Pallas kernels, solve_rows(): pl.pallas_call(functools.partial(solve_kernel, begin, end, step), out_sha...  26.8 us
    all_gather x1, blocking collectives, shards(): lead = lax.all_gather(lead, 'row')  26.2 us
    all_to_all x1, waiting for transfers between devices, shards(): rest = lax.all_to_all(rest, 'col', split_axis=0, concat_axis=0, tiled=True)  19.2 us
    select_n x4, other arithmetic, from_owner_row(): own = jnp.where(away % (2 * stride) == stride, arrived, own)  13.6 us
    pallas_call x2, Pallas kernels, advance(): pl.pallas_call(functools.partial(advance_kernel, count), out_shape=[jax.S...  12.9 us
  transfers between devices with their start and end apart: 10, of which 3 were waited for; matrix products, arithmetic and copies ran while one was open for 12% of the time, Pallas kernels for 32%

profile of v4, /device:TPU:6, one launch (start us, length us, event | category | flops | bytes accessed | tf_op | source)
XLA Modules:
  0.0 414.2 jit_solution(6314816510425342558)
XLA Ops:
  17.7 7.6 %shard_map.60 = bf16[4,2,2,128,16,128]{5,4,3,2,1,0:T(8,128)(2,1)} custom-call(s32[2]{0:T(128)} %pad_add_fusion.2.ids_ref, s32[2,16]{1,0:T(2,128)} %map_ref.3, bf16[2,4,128,16,128]{4,3,2,1,0:T(8,128)(2,1)} %bitcast.127), custom_call_target="tpu_custom_call" | custom-call | tf_op jit(solution)/shard_map/pallas_call | solution.py:123
  28.0 4.7 %fusion.19 = (f32[32,1,128,1,1,128]{5,4,3,2,1,0:T(1,128)}, f32[32,1,128,1,1,128]{5,4,3,2,1,0:T(1,128)}) fusion(f32[32,1,128,16,1,128]{5,4,3,2,1,0:T(1,128)} %param.4), kind=kLoop, calls=%fused_computation.95 | loop fusion | bytes 8388608 | tf_op jit(solution)/shard_map/slice | solution.py:594
  33.8 8.7 %shard_map.61 = (bf16[32,2,128,128]{3,2,1,0:T(8,128)(2,1)}, bf16[32,2,128,128]{3,2,1,0:T(8,128)(2,1)}) custom-call(s32[2,32]{1,0:T(2,128)} %get-tuple-element.130.slot_ref, f32[32,128,128]{2,1,0:T(8,128)} %bitcast.125, f32[32,128,128]{2,1,0:T(8,128)} %bitcast.124, s32[32,2,128]{2,1,0:T(2,128)} %copy.32.refs_2_, bf16[16,128,256]{2,1,0:T(8,128)(2,1)} %bitcast.128), custom_call_target="tpu_custom_call" | custom-call | tf_op jit(solution)/shard_map/pallas_call | solution.py:158
  45.7 36.3 %all-gather.11 = f16[8,4,128,128]{3,2,1,0:T(8,128)(2,1)S(1)} all-gather(f16[1,4,128,128]{3,2,1,0:T(8,128)(2,1)S(1)} %pad_maximum_fusion.2), channel_id=1, replica_groups=mesh['row'=4,'col'=8] {'col'}, dimensions={0}, use_global_device_ids=true | all-gather | bytes 1179648 | tf_op jit(solution)/shard_map/all_gather | solution.py:599
  82.0 26.2 %all-gather.12 = f16[32,4,128,128]{3,2,1,0:T(8,128)(2,1)} all-gather(f16[8,4,128,128]{3,2,1,0:T(8,128)(2,1)S(1)} %all-gather.11), channel_id=2, replica_groups=mesh['row'=4,'col'=8] {'row'}, dimensions={0}, use_global_device_ids=true | all-gather | bytes 5242880 | tf_op jit(solution)/shard_map/all_gather | solution.py:602
  108.2 7.5 %all-to-all-start.1 = ((bf16[4,2,2,128,16,128]{5,4,3,2,1,0:T(8,128)(2,1)}), bf16[4,2,2,128,16,128]{5,4,3,2,1,0:T(8,128)(2,1)}, u32[]{:S(2)}, u32[]{:S(2)}) async-start(bf16[4,2,2,128,16,128]{5,4,3,2,1,0:T(8,128)(2,1)} %shard_map.60), calls=%async_computation.1 | async-start | bytes 16777216 | tf_op jit(solution)/shard_map/all_to_all | solution.py:586
  115.7 6.6 %bitcast_convert_fusion.g_ref = f32[128,128,128]{2,1,0:T(8,128)} fusion(f16[4,8,4,128,128]{4,3,2,1,0:T(8,128)(2,1)} %bitcast.122), kind=kLoop, calls=%fused_computation | loop fusion | flops 2097152 | bytes 12582912 | tf_op jit(solution)/shard_map/convert_element_type | solution.py:605
  122.3 6.3 %shard_map.62 = (f32[512,512]{1,0:T(8,128)}, f32[512,512]{1,0:T(8,128)}, f32[512,512]{1,0:T(8,128)}, f32[512,512]{1,0:T(8,128)}, f32[512,512]{1,0:T(8,128)}, /*index=5*/f32[512,512]{1,0:T(8,128)}) custom-call(f32[128,128,128]{2,1,0:T(8,128)} %bitcast_convert_fusion.g_ref), custom_call_target="tpu_custom_call" | custom-call | tf_op jit(solution)/shard_map/pallas_call | solution.py:200
  132.7 22.7 %shard_map.63 = (f32[512,512]{1,0:T(8,128)}, f32[512,512]{1,0:T(8,128)}, bf16[512,512]{1,0:T(8,128)(2,1)}) custom-call(f32[512,512]{1,0:T(8,128)} %get-tuple-element.53.d_ref), custom_call_target="tpu_custom_call" | custom-call | flops 30000001024 | bytes 4000000 | tf_op jit(solution)/shard_map/pallas_call | solution.py:234
  155.4 8.1 %shard_map.64 = (f32[512,512]{1,0:T(8,128)}, f32[512,512]{1,0:T(8,128)}, bf16[512,512]{1,0:T(8,128)(2,1)}, bf16[512,512]{1,0:T(8,128)(2,1)}, f32[512,512]{1,0:T(...) custom-call(f32[512,512]{1,0:T(8,128)} %get-tuple-element.54.v_ref.refs_6_, f32[512,512]{1,0:T(8,128)} %get-tuple-element.55.refs_0_, ...), custom_call_target="tpu_custom_call" | custom-call | flops 3000000000 | bytes 10000000 | tf_op jit(solution)/shard_map/pallas_call | solution.py:264
  165.5 23.0 %shard_map.65 = (f32[512,512]{1,0:T(8,128)}, f32[512,512]{1,0:T(8,128)}, bf16[512,512]{1,0:T(8,128)(2,1)}) custom-call(f32[512,512]{1,0:T(8,128)} %get-tuple-element.60.d_ref), custom_call_target="tpu_custom_call" | custom-call | flops 30000001024 | bytes 4000000 | tf_op jit(solution)/shard_map/pallas_call | solution.py:234
  188.4 4.8 %shard_map.66 = (f32[512,512]{1,0:T(8,128)}, bf16[512,512]{1,0:T(8,128)(2,1)}, f32[512,512]{1,0:T(8,128)}) custom-call(f32[512,512]{1,0:T(8,128)} %get-tuple-element.61.v_ref.refs_7_, f32[512,512]{1,0:T(8,128)} %get-tuple-element.62.refs_0_, f32[512,512]{1,0:T(8,128)} %get-tuple-element.63.refs_1_), custom_call_target="tpu_custom_call" | custom-call | flops 3000000000 | bytes 10000000 | tf_op jit(solution)/shard_map/pallas_call | solution.py:264
  193.3 5.0 %pad.8 = bf16[8,30,128,128]{3,2,1,0:T(8,128)(2,1)S(1)} pad(bf16[8,29,128,128]{3,2,1,0:T(8,128)(2,1)} %bitcast.113, bf16[]{:T(256)} %constant.142.clone.1), padding=0_0x1_0x0_0x0_0 | pad | bytes 15466498 | tf_op jit(solution)/shard_map/jit(_pad)/pad | solution.py:512
  200.6 6.6 %all-to-all-done.1 = bf16[4,2,2,128,16,128]{5,4,3,2,1,0:T(8,128)(2,1)} async-done(((bf16[4,2,2,128,16,128]{5,4,3,2,1,0:T(8,128)(2,1)}), bf16[4,2,2,128,16,128]{5,4,3,2,1,0:T(8,128)(2,1)}, u32[]{:S(2)}, u32[]{:S(2)}) %all-to-all-start.1) | async-done | bytes 8388640 | tf_op jit(solution)/shard_map/all_to_all | solution.py:586
  210.0 22.7 %shard_map.67 = (f32[512,512]{1,0:T(8,128)}, f32[512,512]{1,0:T(8,128)}, bf16[512,512]{1,0:T(8,128)(2,1)}) custom-call(f32[512,512]{1,0:T(8,128)} %get-tuple-element.68.d_ref), custom_call_target="tpu_custom_call" | custom-call | flops 30000001024 | bytes 4000000 | tf_op jit(solution)/shard_map/pallas_call | solution.py:234
  232.7 13.3 %shard_map.68.refs_4_.refs_16_.refs_17_.refs_18_.refs_19_ = bf16[4096,1024]{1,0:T(8,128)(2,1)} custom-call(bf16[8,29,128,128]{3,2,1,0:T(8,128)(2,1)} %bitcast.114, bf16[8,29,128,128]{3,2,1,0:T(8,128)(2,1)} %bitcast.115, bf16[8,29,128,128]{3,2,1,0:T(8,128)(2,1)} %bitcast.116, bf16[8,29,128,128]{3,2,1,0:T(8,128)(2,1)} %bitcast.117, ...), custom_call_target="tpu_custom_call" | custom-call | flops 8589934592 | bytes 15204352 | tf_op jit(solution)/shard_map/pallas_call | solution.py:383
  246.0 11.7 %all-gather.10.cloned.1.call-done = bf16[120,128,128]{2,1,0:T(8,128)(2,1)} async-done(((bf16[15,128,128]{2,1,0:T(8,128)(2,1)}), bf16[120,128,128]{2,1,0:T(8,128)(2,1)}) %all-gather.10.cloned.1.call-update) | async-done | bytes 3932176 | tf_op jit(solution)/shard_map/all_gather | solution.py:545
  265.0 5.6 %all-to-all-start.2 = ((bf16[8,4,2,128,128]{4,3,1,2,0:T(8,128)(2,1)}), bf16[8,4,2,128,128]{4,3,1,2,0:T(8,128)(2,1)}, u32[]{:S(2)}, u32[]{:S(2)}) async-start(bf16[8,4,2,128,128]{4,3,1,2,0:T(8,128)(2,1)} %copy.38), calls=%async_computation.2 | async-start | bytes 4194304 | tf_op jit(solution)/shard_map/all_to_all | solution.py:663
  275.2 4.4 %broadcast_select_fusion = bf16[8,15,128,128]{3,2,1,0:T(8,128)(2,1)} fusion(bf16[8,15,128,128]{3,2,1,0:T(8,128)(2,1)} %collective-permute-done, bf16[8,15,128,128]{3,2,1,0:T(8,128)(2,1)} %fusion.1, pred[]{:T(512)S(6)} %eq.153), kind=kLoop, calls=%fused_computation.5 | loop fusion | flops 1966080 | bytes 11796481 | tf_op jit(solution)/shard_map/jit(_where)/select_n | solution.py:532
  280.9 13.5 %shard_map.69.refs_20_.refs_21_.refs_22_.refs_23_ = bf16[4096,512]{1,0:T(8,128)(2,1)} custom-call(bf16[4,29,128,128]{3,2,1,0:T(8,128)(2,1)} %pad_maximum_fusion.refs_0_.refs_1_.refs_2_.refs_3_, bf16[4,29,128,128]{3,2,1,0:T(8,128)(2,1)} %pad_maximum_fusion.refs_0_.refs_1_.refs_2_.refs_3_, ...), custom_call_target="tpu_custom_call" | custom-call | flops 6442450944 | bytes 7602176 | tf_op jit(solution)/shard_map/pallas_call | solution.py:383
  300.0 19.2 %all-to-all-done.2 = bf16[8,4,2,128,128]{4,3,1,2,0:T(8,128)(2,1)} async-done(((bf16[8,4,2,128,128]{4,3,1,2,0:T(8,128)(2,1)}), bf16[8,4,2,128,128]{4,3,1,2,0:T(8,128)(2,1)}, u32[]{:S(2)}, u32[]{:S(2)}) %all-to-all-start.2) | async-done | bytes 2097184 | tf_op jit(solution)/shard_map/all_to_all | solution.py:663
  323.7 12.4 %shard_map.71 = f32[512,1536]{1,0:T(8,128)} custom-call(s32[2]{0:T(128)} %pad_add_fusion.2.ids_ref, f32[12,4,128,128]{3,2,1,0:T(8,128)} %pad_maximum_fusion.1.own_ref, f32[512,512]{1,0:T(8,128)} %get-tuple-element.85.refs_0_, f32[512,512]{1,0:T(8,128)} %get-tuple-element.86.refs_1_, f32[512,512]{1,0:T(8,128)} %get-tuple-element.87.refs_2_, ...), custom_call_target="tpu_custom_call" | custom-call | flops 6000000000 | bytes 15000000 | tf_op jit(solution)/shard_map/pallas_call | solution.py:307
  339.2 4.4 %broadcast_select_fusion.1.refs_0_ = bf16[8,15,128,128]{3,2,1,0:T(8,128)(2,1)} fusion(bf16[8,15,128,128]{3,2,1,0:T(8,128)(2,1)} %collective-permute-done.1, bf16[8,15,128,128]{3,2,1,0:T(8,128)(2,1)} %broadcast_select_fusion, pred[]{:T(512)S(6)} %eq.152), kind=kLoop, calls=%fused_computation.6 | loop fusion | flops 1966080 | bytes 11796481 | tf_op jit(solution)/shard_map/jit(_where)/select_n | solution.py:532
  343.6 63.4 %shard_map.70 = f32[65536,128]{1,0:T(8,128)} custom-call(s32[2]{0:T(128)} %pad_add_fusion.2.ids_ref, s32[2,32]{1,0:T(2,128)} %get-tuple-element.131.slot_ref, s32[2,32,128]{2,1,0:T(8,128)} %get-tuple-element.127.order_ref, bf16[8,15,128,128]{3,2,1,0:T(8,128)(2,1)} %broadcast_select_fusion.1.refs_0_, ...), custom_call_target="tpu_custom_call" | custom-call | flops 19327352832 | bytes 67108864 | tf_op jit(solution)/shard_map/pallas_call | solution.py:478
  (71 shorter events, 54.9 us)
Async XLA Ops:
  7.2 10.5 %copy-start.3 = (s32[2,16]{1,0:T(2,128)S(1)}, s32[2,16]{1,0:T(2,128)}, u32[]{:S(2)}) copy-start(s32[2,16]{1,0:T(2,128)} %map_ref.3) | copy-start | bytes 388
  13.6 19.2 %all-to-all-start = ((bf16[4,2,2,128,256]{4,3,2,1,0:T(8,128)(2,1)}), bf16[4,2,2,128,256]{4,3,2,1,0:T(8,128)(2,1)S(1)}, u32[]{:S(2)}, u32[]{:S(2)}) async-start(bf16[4,2,2,128,256]{4,3,2,1,0:T(8,128)(2,1)} %shard_map.59), calls=%async_computation | async-start | bytes 2097152 | tf_op jit(solution)/shard_map/all_to_all | solution.py:586
  17.6 175.6 %all-gather.8.cloned.1.call-start = ((), (), s32[]{:S(2)}) async-start(), calls=%async_computation.3 | async-start | bytes 8552448 | tf_op jit(solution)/shard_map/all_gather | solution.py:545
  17.7 8.1 %copy-start.4 = (s32[2,16,128]{2,1,0:T(8,128)S(1)}, s32[2,16,128]{2,1,0:T(8,128)}, u32[]{:S(2)}) copy-start(s32[2,16,128]{2,1,0:T(8,128)} %param.7) | copy-start | bytes 49156
  32.8 1.0 copy-start.1
  108.2 99.1 %all-to-all-start.1 = ((bf16[4,2,2,128,16,128]{5,4,3,2,1,0:T(8,128)(2,1)}), bf16[4,2,2,128,16,128]{5,4,3,2,1,0:T(8,128)(2,1)}, u32[]{:S(2)}, u32[]{:S(2)}) async-start(bf16[4,2,2,128,16,128]{5,4,3,2,1,0:T(8,128)(2,1)} %shard_map.60), calls=%async_computation.1 | async-start | bytes 16777216 | tf_op jit(solution)/shard_map/all_to_all | solution.py:586
  115.7 142.0 %all-gather.10.cloned.1.call-start = ((), (), s32[]{:S(2)}) async-start(), calls=%async_computation.4 | async-start | bytes 4423680 | tf_op jit(solution)/shard_map/all_gather | solution.py:545
  129.6 33.9 %collective-permute-start.2 = (bf16[15,128,128]{2,1,0:T(8,128)(2,1)S(1)}, bf16[15,128,128]{2,1,0:T(8,128)(2,1)S(1)}, u32[]{:S(2)}, u32[]{:S(2)}) collective-permute-start(bf16[15,128,128]{2,1,0:T(8,128)(2,1)S(1)} %slice_bitcast_fusion.7), channel_id=1, source_target_pairs={{0,4},{1,5},{2,6},{3,7},{8,12},{9,13},{10,14},{11,15},{16,20},{17,... | collective-permute-start | bytes 1474568 | tf_op jit(solution)/shard_map/ppermute | solution.py:543
  207.2 67.9 %collective-permute-start = (bf16[8,15,128,128]{3,2,1,0:T(8,128)(2,1)}, bf16[8,15,128,128]{3,2,1,0:T(8,128)(2,1)}, u32[]{:S(2)}, u32[]{:S(2)}) collective-permute-start(bf16[8,15,128,128]{3,2,1,0:T(8,128)(2,1)} %fusion.1), channel_id=1, source_target_pairs={{0,16},{4,20},{9,25},{13,29},{18,2},{22,6},{27,11},{31,15}} | collective-permute-start | bytes 11796488 | tf_op jit(solution)/shard_map/ppermute | solution.py:529
  261.1 2.3 copy-start.2
  265.0 54.2 %all-to-all-start.2 = ((bf16[8,4,2,128,128]{4,3,1,2,0:T(8,128)(2,1)}), bf16[8,4,2,128,128]{4,3,1,2,0:T(8,128)(2,1)}, u32[]{:S(2)}, u32[]{:S(2)}) async-start(bf16[8,4,2,128,128]{4,3,1,2,0:T(8,128)(2,1)} %copy.38), calls=%async_computation.2 | async-start | bytes 4194304 | tf_op jit(solution)/shard_map/all_to_all | solution.py:663
  273.2 6.4 %copy-start = (bf16[4,15,128,128]{3,2,1,0:T(8,128)(2,1)}, bf16[4,15,128,128]{3,2,1,0:T(8,128)(2,1)S(1)}, u32[]{:S(2)}) copy-start(bf16[4,15,128,128]{3,2,1,0:T(8,128)(2,1)S(1)} %fusion.3) | copy-start | bytes 5898244
  273.2 21.2 %collective-permute-start.3 = (bf16[4,15,128,128]{3,2,1,0:T(8,128)(2,1)S(1)}, bf16[4,15,128,128]{3,2,1,0:T(8,128)(2,1)}, u32[]{:S(2)}, u32[]{:S(2)}) collective-permute-start(bf16[4,15,128,128]{3,2,1,0:T(8,128)(2,1)S(1)} %fusion.3), channel_id=1, source_target_pairs={{0,16},{4,20},{9,25},{13,29},{18,2},{22,6},{27,11},{31,15}} | collective-permute-start | bytes 5898248 | tf_op jit(solution)/shard_map/ppermute | solution.py:529
  279.6 59.6 %collective-permute-start.1 = (bf16[8,15,128,128]{3,2,1,0:T(8,128)(2,1)}, bf16[8,15,128,128]{3,2,1,0:T(8,128)(2,1)}, u32[]{:S(2)}, u32[]{:S(2)}) collective-permute-start(bf16[8,15,128,128]{3,2,1,0:T(8,128)(2,1)} %broadcast_select_fusion), channel_id=1, source_target_pairs={{0,8},{2,10},{4,12},{6,14},{9,1},{11,3},{13,5},{15,7},{16,24},{18,... | collective-permute-start | bytes 11796488 | tf_op jit(solution)/shard_map/ppermute | solution.py:529
  296.2 39.9 %collective-permute-start.4 = (bf16[4,15,128,128]{3,2,1,0:T(8,128)(2,1)S(1)}, bf16[4,15,128,128]{3,2,1,0:T(8,128)(2,1)}, u32[]{:S(2)}, u32[]{:S(2)}) collective-permute-start(bf16[4,15,128,128]{3,2,1,0:T(8,128)(2,1)S(1)} %broadcast_select_fusion.2), channel_id=1, source_target_pairs={{0,8},{2,10},{4,12},{6,14},{9,1},{11,3},{13,5},{15,7},{16,24},{18,... | collective-permute-start | bytes 5898248 | tf_op jit(solution)/shard_map/ppermute | solution.py:529
Sparse Core Ops, SparseCore 0:
  44.8 128.8 all-gather.7
  175.9 81.7 all-gather.9
